TPU v7x, 128 devices: a whole 4x4x4 slice. The times are simulated.
128 devices in a mesh: rep: 16 (over y, x_lo, core), blk: 8 (over z, x_hi).
Axes of the slice: x: 4 (x_hi: 2, x_lo: 2; x = x_hi * 2 + x_lo), y: 4, z: 4, core: 2. Of those that a mesh axis runs over, the one named last changes fastest.
Arguments:
- tokens: bfloat16 [16384, 1536], P(('rep', 'blk')), may hold values from -64 to 64
- attn_in: float32 [1536, 2048], P(('rep', 'blk')), may hold values from -8 to 8
- attn_out: float32 [1536, 1536], P(('rep', 'blk')), may hold values from -0.15625 to 0.15625
- expert_in: float32 [16, 1536, 1536], P(None, ('rep', 'blk')), may hold values from -0.15625 to 0.15625
- expert_out: float32 [16, 768, 1536], P(None, ('rep', 'blk')), may hold values from -0.21875 to 0.21875
- attn_gain: float32 [1536], replicated, may hold values from 0.25 to 1.75
- moe_gain: float32 [1536], replicated, may hold values from 0.25 to 1.75
- lengths: int32 [16, 6], P('rep'), may hold values from 1 to 512, 1024 in all within a row
- page_table: int32 [16, 8], P('rep'), may hold values from 0 to 7, each once within a row
- routes: int32 [16384, 4], P(('rep', 'blk')), may hold values from 0 to 15, all different within a row; in each aligned block of 128 rows (0 to 127, 128 to 255, ...) at most 64 rows name the same one
- gates: bfloat16 [16384, 4], P(('rep', 'blk')), may hold values from 0.19921875 to 1
Outputs:
- mixed: bfloat16 [16384, 1536], P(('rep', 'blk'))
- kv_cache: bfloat16 [128, 128, 512], P(('rep', 'blk'))
Inputs may be any that keep to these rules, and one draw needn't show every extreme that they name: Each replica's lengths sum to 1024. `page_table`: each replica's row is a permutation of its 8 pages. `routes`: a token names 4 different experts; among the rows of one device no expert is named more than 64 times.
All inputs are finite; a program needn't handle non-finite values.
Results may differ from a plain program's by a relative error of at most 0.013.
Values may be sent and summed in bfloat16 or wider, within the bound.
A program may use at most 128 MiB of HBM per device.

v0:
```python
import functools
import math

import jax
import jax.numpy as jnp
from jax import lax
from jax.sharding import PartitionSpec as P

D = 1536
FF = 768
QH = 12
KVH = 2
HD = 128
E = 16
PAGE = 128
CAP = 64
QW = 1536


def rms_scale(values, gain):
    values = values.astype(jnp.float32)
    mean_sq = jnp.mean(values * values, axis=-1, keepdims=True)
    return values * lax.rsqrt(mean_sq + 1e-06) * gain


def rotate(values, position):
    half = values.shape[-1] // 2
    steps_all = jnp.arange(half, dtype=jnp.float32)
    frequency = jnp.exp(steps_all * (-2.0 * math.log(10000.0) / values.shape[-1]))
    angle = position[:, None] * frequency[None, :]
    cosine = jnp.cos(angle)[:, None, :]
    sine = jnp.sin(angle)[:, None, :]
    front = values[..., :half]
    behind = values[..., half:]
    return jnp.concatenate(
        [front * cosine - behind * sine, behind * cosine + front * sine], axis=-1
    )


def segment_info(lengths, count):
    starts = jnp.cumsum(lengths) - lengths
    index = jnp.arange(count, dtype=jnp.int32)
    member = (index[:, None] >= starts[None, :]).astype(jnp.int32)
    segment = jnp.sum(member, axis=1) - 1
    owner = segment[:, None] == jnp.arange(lengths.shape[0], dtype=jnp.int32)[None, :]
    begin = jnp.sum(jnp.where(owner, starts[None, :], 0), axis=1)
    return (segment, index - begin)


def slot_tables(weight, depth):
    member = (weight > 0).astype(jnp.int32)
    ranked = jnp.cumsum(member, axis=0) - 1
    slot_ids = jnp.arange(depth, dtype=jnp.int32)
    hit = (member.T[:, None, :] == 1) & (ranked.T[:, None, :] == slot_ids[None, :, None])
    onehot = hit.astype(jnp.bfloat16)
    gated = jnp.where(hit, weight.T[:, None, :], jnp.zeros((), jnp.bfloat16))
    return (onehot, gated)


def body(
    tokens,
    attn_in,
    attn_out,
    expert_in,
    expert_out,
    attn_gain,
    moe_gain,
    lengths,
    page_table,
    routes,
    gates,
):
    count = tokens.shape[0]
    cycle_size = lax.axis_size("blk")
    place = lax.axis_index("blk")
    group_rows = count * cycle_size
    local_experts = E // cycle_size
    heads_per = QH // KVH
    segment_all, position_all = segment_info(lengths[0], group_rows)
    first = place * count
    my_index = first + jnp.arange(count, dtype=jnp.int32)
    my_segment = lax.dynamic_slice_in_dim(segment_all, first, count)
    my_position = lax.dynamic_slice_in_dim(position_all, first, count).astype(jnp.float32)
    normed = rms_scale(tokens, attn_gain).astype(jnp.bfloat16)
    columns = normed
    projected = jnp.dot(
        columns,
        lax.all_gather(attn_in.astype(jnp.bfloat16), ("rep", "blk"), axis=0, tiled=True),
        preferred_element_type=jnp.float32,
    )
    queries = rotate(projected[:, :QW].reshape(count, QH, HD), my_position).astype(jnp.bfloat16)
    keys_here = rotate(
        projected[:, QW : QW + KVH * HD].reshape(count, KVH, HD), my_position
    ).astype(jnp.bfloat16)
    values_here = projected[:, QW + KVH * HD :].astype(jnp.bfloat16)
    cache_here = jnp.concatenate([keys_here.reshape(count, KVH * HD), values_here], axis=1)
    cache_all = lax.all_gather(cache_here, "blk", axis=0, tiled=True)
    keys_all = cache_all[:, : KVH * HD].reshape(group_rows, KVH, HD)
    values_all = cache_all[:, KVH * HD :].reshape(group_rows, KVH, HD)
    grouped = queries.reshape(count, KVH, heads_per, HD)
    scores = jnp.einsum(
        "igrd,jgd->grij", grouped, keys_all, preferred_element_type=jnp.float32
    ) / math.sqrt(HD)
    key_index = jnp.arange(group_rows, dtype=jnp.int32)
    allowed = (my_segment[:, None] == segment_all[None, :]) & (
        key_index[None, :] <= my_index[:, None]
    )
    scores = jnp.where(allowed[None, None], scores, jnp.float32(-1e30))
    highest = jnp.max(scores, axis=-1, keepdims=True)
    weights = jnp.exp(scores - highest)
    probs = (weights / jnp.sum(weights, axis=-1, keepdims=True)).astype(jnp.bfloat16)
    attended = jnp.einsum("grij,jgd->igrd", probs, values_all, preferred_element_type=jnp.float32)
    attended = attended.astype(jnp.bfloat16).reshape(count, QW)
    columns = attended
    hidden = tokens.astype(jnp.float32) + jnp.dot(
        columns,
        lax.all_gather(attn_out.astype(jnp.bfloat16), ("rep", "blk"), axis=0, tiled=True),
        preferred_element_type=jnp.float32,
    )
    page_count = count // PAGE
    targets = place * page_count + jnp.arange(page_count, dtype=jnp.int32)
    table = page_table[0]
    logical = jnp.sum(
        jnp.where(
            table[None, :] == targets[:, None],
            jnp.arange(table.shape[0], dtype=jnp.int32)[None, :],
            0,
        ),
        axis=1,
    )
    row_ids = logical[:, None] * PAGE + jnp.arange(PAGE, dtype=jnp.int32)[None, :]
    kv_pages = cache_all[row_ids]
    normed_two = rms_scale(hidden, moe_gain).astype(jnp.bfloat16)
    expert_ids = jnp.arange(E, dtype=jnp.int32)
    dense = jnp.sum(
        jnp.where(
            routes[:, :, None] == expert_ids[None, None, :],
            gates.astype(jnp.float32)[:, :, None],
            jnp.float32(0.0),
        ),
        axis=1,
    ).astype(jnp.bfloat16)
    owned_in, owned_out = (
        lax.all_to_all(
            expert_in.astype(jnp.bfloat16), "blk", split_axis=0, concat_axis=1, tiled=True
        ),
        lax.all_to_all(
            expert_out.astype(jnp.bfloat16), "blk", split_axis=0, concat_axis=1, tiled=True
        ),
    )
    rows_all, weight_all = (
        lax.all_gather(normed_two, "blk", axis=0, tiled=True),
        lax.all_gather(dense, "blk", axis=0, tiled=True),
    )
    owned_weight = lax.dynamic_slice_in_dim(weight_all, place * local_experts, local_experts, 1)
    owned_weight = owned_weight.reshape(cycle_size, count, local_experts)
    onehot, gated = jax.vmap(functools.partial(slot_tables, depth=CAP), in_axes=0, out_axes=1)(
        owned_weight
    )
    chosen = jnp.einsum(
        "jsct,stm->jscm",
        onehot,
        rows_all.reshape(cycle_size, count, D),
        preferred_element_type=jnp.float32,
    ).astype(jnp.bfloat16)
    run_chosen = chosen.reshape(local_experts, cycle_size * CAP, D)
    section = run_chosen
    gate_up = jnp.einsum(
        "erd,edf->erf",
        section,
        lax.all_gather(owned_in, "rep", axis=1, tiled=True),
        preferred_element_type=jnp.float32,
    )
    activated = (jax.nn.relu(gate_up[..., :FF]) * gate_up[..., FF:]).astype(jnp.bfloat16)
    section = activated
    summed = jnp.einsum(
        "erf,efd->erd",
        section,
        lax.all_gather(owned_out, "rep", axis=1, tiled=True),
        preferred_element_type=jnp.float32,
    )
    results = summed.astype(jnp.bfloat16)
    results = results.reshape(local_experts, cycle_size, CAP, D)
    summed = jnp.einsum("jsct,jscm->stm", gated, results, preferred_element_type=jnp.float32)
    expert_term = lax.psum_scatter(
        summed.reshape(count * lax.axis_size("blk"), D).astype(jnp.bfloat16),
        "blk",
        scatter_dimension=0,
        tiled=True,
    ).astype(jnp.float32)
    mixed = (hidden + expert_term).astype(jnp.bfloat16)
    return (mixed, kv_pages)


def solution(mesh):
    in_specs = (
        P(("rep", "blk"), None),
        P(("rep", "blk"), None),
        P(("rep", "blk"), None),
        P(None, ("rep", "blk"), None),
        P(None, ("rep", "blk"), None),
        P(),
        P(),
        P("rep", None),
        P("rep", None),
        P(("rep", "blk"), None),
        P(("rep", "blk"), None),
    )
    out_specs = (P(("rep", "blk"), None), P(("rep", "blk"), None, None))
    return jax.shard_map(body, mesh=mesh, in_specs=in_specs, out_specs=out_specs, check_vma=False)
```

profile of v0, /device:TPU:96, one launch (start us, length us, event | category | flops | bytes accessed | tf_op | source)
XLA Modules:
  0.0 959.5 jit_solution(10468634201662940801)
XLA Ops:
  7.2 1.5 convert_bitcast_fusion
  8.8 0.0 all-gather.19.cloned.1.call-start
  8.8 1.5 convert_bitcast_fusion.1
  10.4 0.0 all-gather.9.cloned.1.call-start
  10.4 0.8 reduce-window_clone.1
  11.3 0.7 subtract_bitcast_fusion
  11.9 0.1 convert_reduce_fusion
  12.0 0.1 select_reduce_fusion.1
  12.1 0.1 dynamic-slice_convert_fusion
  12.2 0.2 multiply_cosine_fusion
  12.4 0.1 copy.88
  12.5 0.1 copy.89
  12.6 1.2 fusion.12
  13.8 309.4 %all-gather.17.cloned.1.call-done = bf16[128,12,2048]{2,1,0:T(8,128)(2,1)} async-done(((bf16[1,12,2048]{2,1,0:T(8,128)(2,1)}), bf16[128,12,2048]{2,1,0:T(8,128)(2,1)}) %all-gather.17.cloned.1.call-update) | async-done | bytes 6291472 | tf_op jit(solution)/shard_map/all_gather | solution.py:88
  323.2 10.7 %reshape.228 = bf16[1536,2048]{1,0:T(8,128)(2,1)} reshape(bf16[128,12,2048]{2,1,0:T(8,128)(2,1)} %all-gather.17.cloned.1.call-done) | data formatting | bytes 12582912
  333.9 3.8 fusion.28
  337.8 0.1 reshape.210
  337.8 0.3 subtract_convert_fusion.1
  338.1 0.2 pad_maximum_fusion.2
  338.3 0.7 pad_maximum_fusion.1
  339.1 0.1 dynamic_slice.10
  339.2 0.2 fusion.17
  339.4 297.0 %all-gather.19.cloned.1.call-done = bf16[128,12,1536]{2,1,0:T(8,128)(2,1)} async-done(((bf16[1,12,1536]{2,1,0:T(8,128)(2,1)}), bf16[128,12,1536]{2,1,0:T(8,128)(2,1)}) %all-gather.19.cloned.1.call-update) | async-done | bytes 4718608 | tf_op jit(solution)/shard_map/all_gather | solution.py:117
  636.4 8.2 reshape.230
  644.5 0.1 slice.53
  644.6 0.3 copy.90
  644.9 0.1 subtract_convert_fusion
  645.0 0.2 copy.91
  645.2 0.2 copy.92
  645.5 42.1 %all-gather.9.cloned.1.call-done = bf16[1024,512]{1,0:T(8,128)(2,1)} async-done(((bf16[128,512]{1,0:T(8,128)(2,1)}), bf16[1024,512]{1,0:T(8,128)(2,1)}) %all-gather.9.cloned.1.call-update) | async-done | bytes 1048592 | tf_op jit(solution)/shard_map/all_gather | solution.py:97
  687.6 1.3 fusion.49
  688.9 0.1 reshape.212
  689.0 0.2 copy.113
  689.2 4.8 fusion.50
  694.0 3.5 fusion.11
  697.6 0.4 slice-done.1
  698.0 0.9 multiply_reduce_fusion
  699.0 0.9 copy-done
  699.9 0.9 multiply_convert_fusion
  700.8 0.1 convert_element_type.95
  700.9 0.3 copy.101
  701.3 16.6 %all_to_all.36 = bf16[16,12,1536]{2,1,0:T(8,128)(2,1)S(1)} all-to-all(bf16[16,12,1536]{2,1,0:T(8,128)(2,1)S(1)} %copy.101), channel_id=1, replica_groups=mesh['rep'=16,'blk'=8] {'blk'}, dimensions={0} | all-to-all | bytes 1179648 | tf_op jit(solution)/shard_map/all_to_all | solution.py:144
  717.9 0.6 copy.102
  718.5 0.9 copy.103
  719.5 0.2 copy.104
  719.7 11.9 %all_to_all.37 = bf16[16,6,1536]{2,1,0:T(8,128)(2,1)S(1)} all-to-all(bf16[16,6,1536]{2,1,0:T(8,128)(2,1)S(1)} %copy.104), channel_id=1, replica_groups=mesh['rep'=16,'blk'=8] {'blk'}, dimensions={0} | all-to-all | bytes 589824 | tf_op jit(solution)/shard_map/all_to_all | solution.py:147
  731.6 0.2 copy.105
  731.9 0.8 copy.106
  732.7 0.0 reduce-scatter.2.cloned.1.call-start
  732.8 30.1 %all_gather.24 = bf16[1024,16]{0,1:T(8,128)(2,1)S(1)} all-gather(bf16[128,16]{0,1:T(8,128)(2,1)S(1)} %select_reduce_fusion), channel_id=1, replica_groups=mesh['rep'=16,'blk'=8] {'blk'}, dimensions={0}, use_global_device_ids=true | all-gather | bytes 36864 | tf_op jit(solution)/shard_map/all_gather | solution.py:153
  762.9 0.3 copy.97
  763.2 23.4 %add_bitcast_fusion = s32[2,8,128]{0,1,2:T(8,128)S(1)} fusion(s32[8,128,2]{2,0,1:T(8,128)S(1)} %copy.97), kind=kOutput, calls=%fused_computation.31 | output fusion | flops 262144 | bytes 16384 | tf_op jit(solution)/shard_map/vmap(jit(cumsum))/reduce_window_sum | solution.py:52
  786.5 0.2 copy.98
  786.8 3.0 fusion.2
  789.8 0.3 copy.100
  790.1 31.1 %all-gather.13.cloned.1.call-done = bf16[2,1536,1536]{2,1,0:T(8,128)(2,1)} async-done(((bf16[2,96,1536]{2,1,0:T(8,128)(2,1)}), bf16[2,1536,1536]{2,1,0:T(8,128)(2,1)}) %all-gather.13.cloned.1.call-update) | async-done | bytes 9437200 | tf_op jit(solution)/shard_map/all_gather | solution.py:171
  821.2 10.6 %fusion.55 = f32[2,512,1536]{2,1,0:T(8,128)} fusion(bf16[2,512,1536]{2,1,0:T(8,128)(2,1)S(1)} %bitcast.83, bf16[2,1536,1536]{2,1,0:T(8,128)(2,1)} %all-gather.13.cloned.1.call-done), kind=kOutput, calls=%fused_computation.92 | convolution fusion | flops 4831838208 | bytes 18874368 | tf_op jit(solution)/shard_map/erd,edf->erf/dot_general | solution.py:168
  831.8 30.3 %all-gather.15.cloned.1.call-done = bf16[2,768,1536]{2,1,0:T(8,128)(2,1)} async-done(((bf16[2,48,1536]{2,1,0:T(8,128)(2,1)}), bf16[2,768,1536]{2,1,0:T(8,128)(2,1)}) %all-gather.15.cloned.1.call-update) | async-done | bytes 4718608 | tf_op jit(solution)/shard_map/all_gather | solution.py:179
  862.1 6.8 convolution_convert_fusion
  868.9 2.7 bitcast_convert_fusion
  871.6 0.6 fusion.39
  872.9 1.5 gather_fusion
  874.4 76.4 %reduce-scatter.2.cloned.1.call-done = bf16[128,1536]{1,0:T(8,128)(2,1)} async-done(((bf16[1024,1536]{1,0:T(8,128)(2,1)}), bf16[128,1536]{1,0:T(8,128)(2,1)}) %reduce-scatter.2.cloned.1.call-update) | async-done | bytes 393232 | tf_op jit(solution)/shard_map/reduce_scatter | solution.py:185
  950.8 1.8 add_convert_fusion
  (56 shorter events, 0.5 us)
Async XLA Ops:
  7.2 316.0 %all-gather.17.cloned.1.call-start = ((), (), s32[]{:S(2)}) async-start(), calls=%async_computation.8 | async-start | bytes 8454144 | tf_op jit(solution)/shard_map/all_gather | solution.py:88
  8.8 627.6 %all-gather.19.cloned.1.call-start = ((), (), s32[]{:S(2)}) async-start(), calls=%async_computation.9 | async-start | bytes 6340608 | tf_op jit(solution)/shard_map/all_gather | solution.py:117
  10.4 677.2 %all-gather.9.cloned.1.call-start = ((), (), s32[]{:S(2)}) async-start(), calls=%async_computation.3 | async-start | bytes 1179648 | tf_op jit(solution)/shard_map/all_gather | solution.py:97
  13.8 320.1 %copy-start.3 = (bf16[128,1536]{1,0:T(8,128)(2,1)S(1)}, bf16[128,1536]{1,0:T(8,128)(2,1)}, u32[]{:S(2)}) copy-start(bf16[128,1536]{1,0:T(8,128)(2,1)} %param.11) | copy-start | bytes 1179652
  13.8 320.1 %copy-start.6 = (f32[1536]{0:T(1024)S(1)}, f32[1536]{0:T(1024)}, u32[]{:S(2)}) copy-start(f32[1536]{0:T(1024)} %param.16) | copy-start | bytes 18436
  339.0 447.8 %all-gather.11.cloned.1.call-start = ((), (), s32[]{:S(2)}) async-start(), calls=%async_computation.4 | async-start | bytes 3538944 | tf_op jit(solution)/shard_map/all_gather | solution.py:152
  689.2 8.4 slice-start
  694.0 4.0 slice-start.1
  697.6 2.3 copy-start.7
  697.6 3.2 copy-start.4
  698.9 0.9 copy-start
  699.9 19.6 %copy-start.5 = (f32[16,6,1536]{2,0,1:T(8,128)S(1)}, f32[16,6,1536]{2,0,1:T(8,128)}, u32[]{:S(2)}) copy-start(f32[16,6,1536]{2,0,1:T(8,128)} %param.15) | copy-start | bytes 1769476
  700.8 120.4 %all-gather.13.cloned.1.call-start = ((), (), s32[]{:S(2)}) async-start(), calls=%async_computation.5 | async-start | bytes 10027008 | tf_op jit(solution)/shard_map/all_gather | solution.py:171
  700.9 31.8 %copy-start.9 = (bf16[128,4]{0,1:T(4,128)(2,1)S(1)}, bf16[128,4]{0,1:T(4,128)(2,1)}, u32[]{:S(2)}) copy-start(bf16[128,4]{0,1:T(4,128)(2,1)} %param.21) | copy-start | bytes 3076
  700.9 31.8 %copy-start.8 = (s32[128,4]{0,1:T(4,128)S(1)}, s32[128,4]{0,1:T(4,128)}, u32[]{:S(2)}) copy-start(s32[128,4]{0,1:T(4,128)} %param.20) | copy-start | bytes 6148
  719.4 142.6 %all-gather.15.cloned.1.call-start = ((), (), s32[]{:S(2)}) async-start(), calls=%async_computation.6 | async-start | bytes 5013504 | tf_op jit(solution)/shard_map/all_gather | solution.py:179
  732.7 218.1 %reduce-scatter.2.cloned.1.call-start = ((), (), s32[]{:S(2)}) async-start(), calls=%async_computation.7 | async-start | bytes 3538944 | tf_op jit(solution)/shard_map/reduce_scatter | solution.py:185
  868.9 2.7 copy-start.10
  868.9 4.0 copy-start.2
  868.9 81.9 %copy-start.1 = (f32[128,1536]{1,0:T(8,128)S(1)}, f32[128,1536]{1,0:T(8,128)}, u32[]{:S(2)}) copy-start(f32[128,1536]{1,0:T(8,128)} %copy-done) | copy-start | bytes 2359300
Sparse Core Ops, SparseCore 0:
  10.3 312.8 all-gather.16
  325.4 310.8 all-gather.18
  639.3 48.2 all-gather.8
  700.9 61.7 all-gather.10
  764.1 57.0 all-gather.12
  822.7 39.3 all-gather.14
  871.7 79.0 reduce-scatter.1
where the time goes:
time: 962 us; the launch traced here: 959 us
  waiting for transfers between devices  786 us (82%)
  blocking collectives  58.7 us (6%)
  matrix products  36.1 us (4%)
  other arithmetic  34.5 us (4%)
  local copies, waits for them, and re-layouts  28.3 us (3%)
  between operations  15.2 us (2%)
    all_gather x1, waiting for transfers between devices, body(): lax.all_gather(attn_in.astype(jnp.bfloat16), ('rep', 'blk'), axis=0, tile...  309 us
    all_gather x1, waiting for transfers between devices, body(): lax.all_gather(attn_out.astype(jnp.bfloat16), ('rep', 'blk'), axis=0, til...  297 us
    reduce_scatter x1, waiting for transfers between devices, body(): lax.psum_scatter(summed.reshape(count * lax.axis_size('blk'), D).astype(j...  76.4 us
    all_gather x1, waiting for transfers between devices, body(): cache_all = lax.all_gather(cache_here, 'blk', axis=0, tiled=True)  42.1 us
    all_gather x1, waiting for transfers between devices, body(): lax.all_gather(owned_in, 'rep', axis=1, tiled=True)  31.1 us
    all_gather x1, waiting for transfers between devices, body(): lax.all_gather(owned_out, 'rep', axis=1, tiled=True)  30.3 us
    all_gather x1, blocking collectives, body(): lax.all_gather(dense, 'blk', axis=0, tiled=True)  30.1 us
    another operation x1, other arithmetic, slot_tables(): ranked = jnp.cumsum(member, axis=0) - 1  23.4 us
  transfers between devices with their start and end apart: 7, of which 6 were waited for; matrix products, arithmetic and copies ran while one was open for 8% of the time, Pallas kernels for 0%

commit v1 on v0

--- a/solution.py
+++ b/solution.py
@@ -4,6 +4,8 @@
 import jax
 import jax.numpy as jnp
 from jax import lax
+from jax.experimental import pallas as pl
+from jax.experimental.pallas import tpu as pltpu
 from jax.sharding import PartitionSpec as P
 
 D = 1536
@@ -15,6 +17,9 @@
 PAGE = 128
 CAP = 64
 QW = 1536
+BF = jnp.bfloat16
+F32 = jnp.float32
+MESH = pl.DeviceIdType.MESH
 
 
 def rms_scale(values, gain):
@@ -55,6 +60,267 @@
     onehot = hit.astype(jnp.bfloat16)
     gated = jnp.where(hit, weight.T[:, None, :], jnp.zeros((), jnp.bfloat16))
     return (onehot, gated)
+
+
+class Net:
+    def __init__(self, send_sems, recv_sems):
+        rep, blk = lax.axis_index("rep"), lax.axis_index("blk")
+        self.y, self.xl, self.c = rep // 4, (rep // 2) % 2, rep % 2
+        self.z, self.xh = blk // 2, blk % 2
+        self.x = self.xh * 2 + self.xl
+        self.ss, self.rs, self.used = send_sems, recv_sems, 0
+
+    def dev(self, y=0, x=0, z=0, c=0):
+        yy = (self.y + y) % 4
+        xx = (self.x + x) % 4
+        zz = (self.z + z) % 4
+        cc = (self.c + c) % 2
+        return ((yy * 2 + xx % 2) * 2 + cc, zz * 2 + xx // 2)
+
+    def xflip(self):
+        return (((self.y * 2 + 1 - self.xl) * 2) + self.c, self.z * 2 + self.xh)
+
+    def take(self, n=1):
+        k = self.used
+        self.used = k + n
+        return k
+
+    def make(self, src, dst, to, k):
+        return pltpu.make_async_remote_copy(
+            src_ref=src,
+            dst_ref=dst,
+            send_sem=self.ss.at[k],
+            recv_sem=self.rs.at[k],
+            device_id=to,
+            device_id_type=MESH,
+        )
+
+    def send(self, ref, to):
+        cp = self.make(ref, ref, to, self.take())
+        cp.start()
+        return cp
+
+
+def enter(net):
+    barrier = pltpu.get_barrier_semaphore()
+    around = [net.dev(x=1), net.dev(x=3), net.dev(c=1)]
+    around += [net.dev(y=k) for k in (1, 2, 3)]
+    around += [net.dev(z=dz, x=dx) for dz in range(4) for dx in (0, 2) if dz or dx]
+    for to in around:
+        pl.semaphore_signal(barrier, inc=1, device_id=to, device_id_type=MESH)
+    pl.semaphore_wait(barrier, len(around))
+
+
+def gather_weights(net, qs, ms, es, os, q1, m1, e1, o1, wq, wm, wi, wo):
+    y, xl, c, z, xh = net.y, net.xl, net.c, net.z, net.xh
+    sent = []
+    half = z // 2
+    slot = (z % 2) * 2 + xh
+    first = {}
+    for name, src, dst in (("q", qs, q1), ("m", ms, m1)):
+        base_s, base_r = net.take(4), net.used - 4
+        for k in range(4):
+            zt = (z + k) % 4
+            cp = pltpu.make_async_remote_copy(
+                src_ref=src.at[zt],
+                dst_ref=dst.at[slot],
+                send_sem=net.ss.at[base_s + k],
+                recv_sem=net.rs.at[base_r + slot],
+                device_id=((y * 2 + xl) * 2 + c, zt * 2 + half),
+                device_id_type=MESH,
+            )
+            if k == 0:
+
+                @pl.when(half != xh)
+                def _(cp=cp):
+                    cp.start()
+
+                @pl.when(half == xh)
+                def _(src=src, dst=dst):
+                    dst[pl.ds(slot, 1)] = src[pl.ds(z, 1)]
+
+            else:
+                cp.start()
+            first[name, k] = cp
+    blk = z * 2 + xh
+    for name, src, dst in (("e", es, e1), ("o", os, o1)):
+        base = net.take(8)
+        for k in range(1, 8):
+            to = (blk + k) % 8
+            cp = pltpu.make_async_remote_copy(
+                src_ref=src.at[pl.ds(2 * to, 2)],
+                dst_ref=dst.at[blk],
+                send_sem=net.ss.at[base + k],
+                recv_sem=net.rs.at[base + k],
+                device_id=((y * 2 + xl) * 2 + c, to),
+                device_id_type=MESH,
+            )
+            cp.start()
+            first[name, k] = cp
+        dst[pl.ds(blk, 1)] = src[pl.ds(2 * blk, 2)][None]
+
+    def wait_first(name, src, dst, base):
+        for j in range(4):
+            mine = (z == 2 * xh + j // 2) & (xh == j % 2)
+
+            @pl.when(jnp.logical_not(mine))
+            def _(j=j):
+                net.make(src.at[0], dst.at[0], net.dev(c=1), base + j).wait_recv()
+
+    def stack(pieces):
+        return jnp.concatenate([p.astype(F32) for p in pieces], axis=0).astype(BF)
+
+    wait_first("q", qs, q1, 0)
+    block = stack([q1[j] for j in range(4)])
+    ca = pl.ds(pl.multiple_of(z * 256, 256), 256)
+    cb = pl.ds(pl.multiple_of(1024 + z * 256, 256), 256)
+    cm = pl.ds(pl.multiple_of(z * 384, 128), 384)
+    wq[y, xl, c, xh, :, ca] = block[:, :256]
+    wq[y, xl, c, xh, :, cb] = block[:, 256:]
+    wait_first("m", ms, m1, 4)
+    wm[y, xl, c, xh, :, cm] = stack([m1[j] for j in range(4)])
+    xs = (1, 3, 2)
+    q2 = [net.send(wq.at[y, xl, c, xh, :, col], net.dev(x=k)) for k in xs for col in (ca, cb)]
+    m2 = [net.send(wm.at[y, xl, c, xh, :, cm], net.dev(x=k)) for k in xs]
+    for cp in q2:
+        cp.wait_recv()
+    q3a = [net.send(wq.at[y, :, c, :, :, ca], net.dev(y=k)) for k in xs]
+    q3b = [net.send(wq.at[y, :, c, :, :, cb], net.dev(z=k)) for k in xs]
+    for cp in m2:
+        cp.wait_recv()
+    m3 = [net.send(wm.at[y, :, c, :, :, cm], net.dev(y=k)) for k in xs]
+    for cp in q3a:
+        cp.wait_recv()
+    q4a = [net.send(wq.at[:, :, c, :, :, ca], net.dev(z=k)) for k in xs]
+    for cp in q3b:
+        cp.wait_recv()
+    cbb = pl.ds(1024, 1024)
+    q4b = [net.send(wq.at[y, :, c, :, :, cbb], net.dev(y=k)) for k in xs]
+    q5 = [
+        net.send(wq.at[:, :, c, :, :, ca], net.dev(c=1)),
+        net.send(wq.at[y, :, c, :, :, cbb], net.dev(c=1)),
+    ]
+    sent += q2 + m2 + q3a + q3b + m3 + q4a + q4b
+    for k in range(1, 8):
+        first["e", k].wait_recv()
+
+    def lay(src, dst, rows, width):
+        def step(i, carry):
+            col = pl.ds(pl.multiple_of(i * width, width), width)
+            for e in range(2):
+                dst[e, y, xl, c, :, col] = stack([src[j, e, :, col] for j in range(8)])
+            return carry
+
+        lax.fori_loop(0, D // width, step, 0)
+
+    lay(e1, wi, 96, 256)
+    i1 = net.send(wi.at[:, y, xl, c], net.xflip())
+    i2 = {k: net.send(wi.at[:, y, xl, c], net.dev(y=k)) for k in (1, 3)}
+    for k in range(1, 8):
+        first["o", k].wait_recv()
+    lay(o1, wo, 48, 256)
+    u1 = {k: net.send(wo.at[:, y, xl, c], net.dev(y=k)) for k in (1, 3, 2)}
+    p5 = [net.send(wi.at[:, y, xl, c], net.dev(c=1)), net.send(wo.at[:, y, xl, c], net.dev(c=1))]
+    u2 = [net.send(wo.at[:, y, xl, c], net.xflip())]
+    sent += [i1, *i2.values(), *u1.values(), *p5, *u2]
+    for cp in m3:
+        cp.wait_recv()
+    m4 = [net.send(wm.at[:, :, c, :, :, cm], net.dev(z=k)) for k in xs]
+    m5 = [net.send(wm.at[:, :, c, :, :, cm], net.dev(c=1))]
+    sent += m4
+    i1.wait_recv()
+    i3 = {k: net.send(wi.at[:, y, 1 - xl, c], net.dev(y=k)) for k in (1, 3)}
+    p5b = [net.send(wi.at[:, y, 1 - xl, c], net.dev(c=1))]
+    sent += [*i3.values(), *p5b]
+    for n, k in enumerate(xs):
+        q4a[n].wait_recv()
+        zf = (z + 4 - k) % 4
+        q5.append(
+            net.send(
+                wq.at[:, :, c, :, :, pl.ds(pl.multiple_of(zf * 256, 256), 256)], net.dev(c=1)
+            )
+        )
+        q4b[n].wait_recv()
+        q5.append(net.send(wq.at[(y + 4 - k) % 4, :, c, :, :, cbb], net.dev(c=1)))
+    sent += q5
+    recv = list(q5)
+    up, down = net.dev(y=1), net.dev(y=3)
+    lo, hi = (y + 3) % 4, (y + 1) % 4
+    for k in (1, 3):
+        i2[k].wait_recv()
+    for k in (1, 3):
+        i3[k].wait_recv()
+    r4 = [net.send(wi.at[:, lo, 0, c], up), net.send(wi.at[:, hi, 1, c], down)]
+    p6 = [net.send(wi.at[:, lo, :, c], net.dev(c=1)), net.send(wi.at[:, hi, :, c], net.dev(c=1))]
+    for n, k in enumerate(xs):
+        u1[k].wait_recv()
+        yf = (y + 4 - k) % 4
+        u2.append(net.send(wo.at[:, yf, xl, c], net.xflip()))
+        p6.append(net.send(wo.at[:, yf, xl, c], net.dev(c=1)))
+        sent += u2[-1:]
+    for n, k in enumerate(xs):
+        m4[n].wait_recv()
+        zf = (z + 4 - k) % 4
+        m5.append(
+            net.send(
+                wm.at[:, :, c, :, :, pl.ds(pl.multiple_of(zf * 384, 128), 384)], net.dev(c=1)
+            )
+        )
+    sent += m5
+    recv += m5
+    for n, k in enumerate((0,) + xs):
+        u2[n].wait_recv()
+        p6.append(net.send(wo.at[:, (y + 4 - k) % 4, 1 - xl, c], net.dev(c=1)))
+    for cp in r4:
+        cp.wait_recv()
+    p6.append(net.send(wi.at[:, (y + 2) % 4, :, c], net.dev(c=1)))
+    sent += r4 + p6
+    recv += p5 + p5b + p6
+    for cp in recv:
+        cp.wait_recv()
+    for (name, k), cp in first.items():
+        if k:
+            cp.wait_send()
+        else:
+
+            @pl.when(half != xh)
+            def _(cp=cp):
+                cp.wait_send()
+
+    for cp in sent:
+        cp.wait_send()
+
+
+def weights_kernel(qs, ms, es, os, wq, wm, wi, wo, q1, m1, e1, o1, ss, rs):
+    net = Net(ss, rs)
+    enter(net)
+    gather_weights(net, qs, ms, es, os, q1, m1, e1, o1, wq, wm, wi, wo)
+
+
+def weights_call(qs, ms, es, os):
+    vm = pl.BlockSpec(memory_space=pltpu.VMEM)
+    return pl.pallas_call(
+        weights_kernel,
+        out_shape=(
+            jax.ShapeDtypeStruct((4, 2, 2, 2, 48, 2048), BF),
+            jax.ShapeDtypeStruct((4, 2, 2, 2, 48, D), BF),
+            jax.ShapeDtypeStruct((2, 4, 2, 2, 96, D), BF),
+            jax.ShapeDtypeStruct((2, 4, 2, 2, 48, D), BF),
+        ),
+        in_specs=[vm] * 4,
+        out_specs=(vm,) * 4,
+        scratch_shapes=[
+            pltpu.VMEM((4, 12, 512), BF),
+            pltpu.VMEM((4, 12, 384), BF),
+            pltpu.VMEM((8, 2, 12, D), BF),
+            pltpu.VMEM((8, 2, 6, D), BF),
+            pltpu.SemaphoreType.DMA((120,)),
+            pltpu.SemaphoreType.DMA((120,)),
+        ],
+        compiler_params=pltpu.CompilerParams(
+            collective_id=0, has_side_effects=True, vmem_limit_bytes=60 << 20
+        ),
+    )(qs, ms, es, os)
 
 
 def body(
@@ -76,18 +342,18 @@
     group_rows = count * cycle_size
     local_experts = E // cycle_size
     heads_per = QH // KVH
+    qs = attn_in.astype(BF).reshape(12, 2, 4, 256).transpose(2, 0, 1, 3).reshape(4, 12, 512)
+    ms = attn_out.astype(BF).reshape(12, 4, 384).transpose(1, 0, 2)
+    wq, wm, wi, wo = weights_call(qs, ms, expert_in.astype(BF), expert_out.astype(BF))
+    wq, wm = wq.reshape(D, 2048), wm.reshape(D, D)
+    wi, wo = wi.reshape(2, D, D), wo.reshape(2, FF, D)
     segment_all, position_all = segment_info(lengths[0], group_rows)
     first = place * count
     my_index = first + jnp.arange(count, dtype=jnp.int32)
     my_segment = lax.dynamic_slice_in_dim(segment_all, first, count)
     my_position = lax.dynamic_slice_in_dim(position_all, first, count).astype(jnp.float32)
     normed = rms_scale(tokens, attn_gain).astype(jnp.bfloat16)
-    columns = normed
-    projected = jnp.dot(
-        columns,
-        lax.all_gather(attn_in.astype(jnp.bfloat16), ("rep", "blk"), axis=0, tiled=True),
-        preferred_element_type=jnp.float32,
-    )
+    projected = jnp.dot(normed, wq, preferred_element_type=jnp.float32)
     queries = rotate(projected[:, :QW].reshape(count, QH, HD), my_position).astype(jnp.bfloat16)
     keys_here = rotate(
         projected[:, QW : QW + KVH * HD].reshape(count, KVH, HD), my_position
@@ -111,11 +377,8 @@
     probs = (weights / jnp.sum(weights, axis=-1, keepdims=True)).astype(jnp.bfloat16)
     attended = jnp.einsum("grij,jgd->igrd", probs, values_all, preferred_element_type=jnp.float32)
     attended = attended.astype(jnp.bfloat16).reshape(count, QW)
-    columns = attended
     hidden = tokens.astype(jnp.float32) + jnp.dot(
-        columns,
-        lax.all_gather(attn_out.astype(jnp.bfloat16), ("rep", "blk"), axis=0, tiled=True),
-        preferred_element_type=jnp.float32,
+        attended, wm, preferred_element_type=jnp.float32
     )
     page_count = count // PAGE
     targets = place * page_count + jnp.arange(page_count, dtype=jnp.int32)
@@ -140,14 +403,6 @@
         ),
         axis=1,
     ).astype(jnp.bfloat16)
-    owned_in, owned_out = (
-        lax.all_to_all(
-            expert_in.astype(jnp.bfloat16), "blk", split_axis=0, concat_axis=1, tiled=True
-        ),
-        lax.all_to_all(
-            expert_out.astype(jnp.bfloat16), "blk", split_axis=0, concat_axis=1, tiled=True
-        ),
-    )
     rows_all, weight_all = (
         lax.all_gather(normed_two, "blk", axis=0, tiled=True),
         lax.all_gather(dense, "blk", axis=0, tiled=True),
@@ -163,22 +418,10 @@
         rows_all.reshape(cycle_size, count, D),
         preferred_element_type=jnp.float32,
     ).astype(jnp.bfloat16)
-    run_chosen = chosen.reshape(local_experts, cycle_size * CAP, D)
-    section = run_chosen
-    gate_up = jnp.einsum(
-        "erd,edf->erf",
-        section,
-        lax.all_gather(owned_in, "rep", axis=1, tiled=True),
-        preferred_element_type=jnp.float32,
-    )
+    section = chosen.reshape(local_experts, cycle_size * CAP, D)
+    gate_up = jnp.einsum("erd,edf->erf", section, wi, preferred_element_type=jnp.float32)
     activated = (jax.nn.relu(gate_up[..., :FF]) * gate_up[..., FF:]).astype(jnp.bfloat16)
-    section = activated
-    summed = jnp.einsum(
-        "erf,efd->erd",
-        section,
-        lax.all_gather(owned_out, "rep", axis=1, tiled=True),
-        preferred_element_type=jnp.float32,
-    )
+    summed = jnp.einsum("erf,efd->erd", activated, wo, preferred_element_type=jnp.float32)
     results = summed.astype(jnp.bfloat16)
     results = results.reshape(local_experts, cycle_size, CAP, D)
     summed = jnp.einsum("jsct,jscm->stm", gated, results, preferred_element_type=jnp.float32)

time: 962 us -> 373 us (0.39)
  waiting for transfers between devices: 786 us -> 130 us
  Pallas kernels: 0 us -> 123 us
  blocking collectives: 58.7 us -> 28.5 us
  local copies, waits for them, and re-layouts: 28.3 us -> 8.67 us
    all_gather x4 -> x0, waiting for transfers between devices: 668 us -> none  [the longest x1 309 us: body(): lax.all_gather(attn_in.astype(jnp.bfloat16), ('rep', 'blk'), axis=0, tile...]
    pallas_call x0 -> x1, Pallas kernels: none -> 123 us  [weights_call(): pl.pallas_call(weights_kernel, out_shape=(jax.ShapeDtypeStruct((4, 2, 2,...]
    all_to_all x2 -> x0, blocking collectives: 28.6 us -> none  [the longest x1 16.6 us: body(): lax.all_to_all(expert_in.astype(jnp.bfloat16), 'blk', split_axis=0, conca...]
    unnamed x31 -> x23, local copies, waits for them, and re-layouts: 20.3 us -> 0.08 us
  transfers between devices with their start and end apart: 7 -> 3, of which waited for: 6 -> 3; matrix products, arithmetic and copies ran while one was open for 8% -> 7% of each run, Pallas kernels for 0% -> 0%
where the time goes in v1:
time: 373 us; the launch traced here: 371 us
  waiting for transfers between devices  130 us (35%)
  Pallas kernels  123 us (33%)
  other arithmetic  34.3 us (9%)
  matrix products  31.4 us (8%)
  blocking collectives  28.5 us (8%)
  between operations  14.9 us (4%)
  local copies, waits for them, and re-layouts  8.67 us (2%)
    pallas_call x1, Pallas kernels, weights_call(): pl.pallas_call(weights_kernel, out_shape=(jax.ShapeDtypeStruct((4, 2, 2,...  123 us
    reduce_scatter x1, waiting for transfers between devices, body(): lax.psum_scatter(summed.reshape(count * lax.axis_size('blk'), D).astype(j...  76.2 us
    all_gather x1, waiting for transfers between devices, body(): cache_all = lax.all_gather(cache_here, 'blk', axis=0, tiled=True)  46 us
    all_gather x1, blocking collectives, body(): lax.all_gather(dense, 'blk', axis=0, tiled=True)  28.5 us
    another operation x1, other arithmetic, slot_tables(): ranked = jnp.cumsum(member, axis=0) - 1  23.4 us
    dot_general x1, matrix products, body(): jnp.einsum('erd,edf->erf', section, wi, preferred_element_type=jnp.float32)  7.76 us
    all_gather x1, waiting for transfers between devices, body(): lax.all_gather(normed_two, 'blk', axis=0, tiled=True)  7.58 us
  transfers between devices with their start and end apart: 3, of which 3 were waited for; matrix products, arithmetic and copies ran while one was open for 7% of the time, Pallas kernels for 0%

profile of v1, /device:TPU:96, one launch (start us, length us, event | category | flops | bytes accessed | tf_op | source)
XLA Modules:
  0.0 370.9 jit_solution(11247719535282666937)
XLA Ops:
  7.2 0.0 copy-start.1
  7.2 0.0 all-gather.3.cloned.1.call-start
  7.2 1.2 fusion.12
  8.5 0.9 convert_element_type.82
  9.4 0.6 copy.118
  10.0 0.9 convert_element_type.81
  11.1 0.6 copy.69.qs
  11.7 1.1 convert_element_type.84
  12.8 0.9 copy.71.os
  13.7 1.3 convert_element_type.83
  15.1 1.3 copy.70.es
  16.3 123.2 %shard_map.122 = (bf16[4,2,2,2,48,2048]{5,4,3,2,1,0:T(8,128)(2,1)}, bf16[4,2,2,2,48,1536]{5,4,3,2,1,0:T(8,128)(2,1)}, bf16[2,4,2,2,96,1536]{5,4,3,2,1,0:T(8,128)(2,1)}, bf16[2,4,2,2,48,1536]{5,4,3,2,1,0:T(8,128)(2,1)}) custom-call(bf16[4,12,512]{2,1,0:T(8,128)(2,1)} %copy.69.qs, bf16[4,12,384]{2,1,0:T(8,128)(2,1)} %bitcast.98, ...), custom_call_target="tpu_custom_call" | custom-call | tf_op jit(solution)/shard_map/pallas_call | solution.py:302
  139.6 3.8 %fusion.28 = f32[128,2048]{1,0:T(8,128)S(1)} fusion(bf16[1536,2048]{1,0:T(8,128)(2,1)} %bitcast.86, bf16[128,1536]{1,0:T(8,128)(2,1)S(1)} %copy-done.1, f32[1536]{0:T(1024)S(1)} %copy-done.2, f32[128]{0:T(128)S(1)} %add_rsqrt_fusion.1), kind=kOutput, calls=%fused_computation.39 | convolution fusion | flops 806092800 | bytes 7739904 | tf_op jit(solution)/shard_map/dot_general | solution.py:356
  143.4 0.2 reduce-window_clone.1
  143.6 0.1 convert_reduce_fusion
  143.7 0.1 select_reduce_fusion.1
  143.8 0.1 dynamic-slice_convert_fusion
  143.9 0.2 multiply_cosine_fusion
  144.1 0.1 copy.72
  144.2 0.1 copy.73
  144.3 0.1 reshape.235
  144.4 0.3 subtract_convert_fusion.1
  144.7 0.2 pad_maximum_fusion.2
  144.9 0.7 pad_maximum_fusion.1
  145.5 0.0 all-gather.3.cloned.1.call-update
  145.6 0.0 all-gather.5.cloned.1.call-start
  145.6 0.1 dynamic_slice.10
  145.7 0.1 slice.53
  145.8 0.3 copy.74
  146.0 0.1 subtract_convert_fusion
  146.2 0.2 copy.75
  146.4 0.2 copy.76
  146.7 0.2 fusion.17
  146.9 46.0 %all-gather.3.cloned.1.call-done = bf16[1024,512]{1,0:T(8,128)(2,1)} async-done(((bf16[128,512]{1,0:T(8,128)(2,1)}), bf16[1024,512]{1,0:T(8,128)(2,1)}) %all-gather.3.cloned.1.call-update) | async-done | bytes 1048592 | tf_op jit(solution)/shard_map/all_gather | solution.py:363
  192.9 1.3 fusion.49
  194.1 0.1 reshape.237
  194.3 0.2 copy.91
  194.5 4.8 %fusion.50 = (f32[2,6,128]{2,1,0:T(8,128)S(1)}, f32[2,6,128,1024]{2,3,1,0:T(8,128)}) fusion(pred[128,1024]{0,1:T(8,128)(4,1)S(1)} %fusion.17, bf16[1024,2,128,1]{2,1,0,3:T(2,128)(2,1)S(1)} %bitcast.91, bf16[128,2,6,64]{3,0,2,1:T(8,128)(2,1)S(1)} %bitcast.95, bf16[128,2,6,64]{3,0,2,1:T(8,128)(2,1)S(1)} %bitcast.94), kind=kOutput, calls=%fused_computation.91 | convolution fusion | flops 409732096 | bytes 7346176 | tf_op jit(solution)/shard_map/sub | solution.py:376
  199.3 3.4 fusion.11
  202.7 0.0 copy-start.3
  202.7 0.0 copy-start.5
  202.7 0.0 copy-start.4
  202.7 3.2 multiply_reduce_fusion
  206.0 0.9 multiply_convert_fusion
  206.9 0.0 all-gather.5.cloned.1.call-update
  206.9 0.0 reduce-scatter.2.cloned.1.call-start
  207.0 28.5 %all_gather.10 = bf16[1024,16]{0,1:T(8,128)(2,1)S(1)} all-gather(bf16[128,16]{0,1:T(8,128)(2,1)S(1)} %select_reduce_fusion), channel_id=1, replica_groups=mesh['rep'=16,'blk'=8] {'blk'}, dimensions={0}, use_global_device_ids=true | all-gather | bytes 36864 | tf_op jit(solution)/shard_map/all_gather | solution.py:408
  235.6 0.3 copy.81
  235.9 23.4 %add_bitcast_fusion = s32[2,8,128]{0,1,2:T(8,128)S(1)} fusion(s32[8,128,2]{2,0,1:T(8,128)S(1)} %copy.81), kind=kOutput, calls=%fused_computation.31 | output fusion | flops 262144 | bytes 16384 | tf_op jit(solution)/shard_map/vmap(jit(cumsum))/reduce_window_sum | solution.py:57
  259.3 0.2 copy.82
  259.5 7.6 %all-gather.5.cloned.1.call-done = bf16[1024,1536]{1,0:T(8,128)(2,1)} async-done(((bf16[128,1536]{1,0:T(8,128)(2,1)}), bf16[1024,1536]{1,0:T(8,128)(2,1)}) %all-gather.5.cloned.1.call-update) | async-done | bytes 3145744 | tf_op jit(solution)/shard_map/all_gather | solution.py:407
  267.0 2.9 fusion.2
  269.9 0.0 slice-start
  269.9 0.3 copy.84
  270.2 0.0 slice-start.1
  270.2 7.8 %fusion.55 = f32[2,512,1536]{2,1,0:T(8,128)S(1)} fusion(bf16[2,512,1536]{2,1,0:T(8,128)(2,1)S(1)} %bitcast.83, bf16[2,1536,1536]{2,1,0:T(8,128)(2,1)} %bitcast.85), kind=kOutput, calls=%fused_computation.92 | convolution fusion | flops 4831838208 | bytes 18874368 | tf_op jit(solution)/shard_map/erd,edf->erf/dot_general | solution.py:422
  278.0 2.8 convolution_convert_fusion
  280.8 0.0 copy-start.7
  280.8 2.7 bitcast_convert_fusion
  283.5 0.0 reduce-scatter.2.cloned.1.call-update
  283.6 0.6 fusion.39
  284.9 1.5 gather_fusion
  286.4 76.2 %reduce-scatter.2.cloned.1.call-done = bf16[128,1536]{1,0:T(8,128)(2,1)} async-done(((bf16[1024,1536]{1,0:T(8,128)(2,1)}), bf16[128,1536]{1,0:T(8,128)(2,1)}) %reduce-scatter.2.cloned.1.call-update) | async-done | bytes 393232 | tf_op jit(solution)/shard_map/reduce_scatter | solution.py:428
  362.6 1.8 add_convert_fusion
  (37 shorter events, 0.3 us)
Async XLA Ops:
  7.2 132.4 %copy-start.1 = (bf16[128,1536]{1,0:T(8,128)(2,1)S(1)}, bf16[128,1536]{1,0:T(8,128)(2,1)}, u32[]{:S(2)}) copy-start(bf16[128,1536]{1,0:T(8,128)(2,1)} %param.11) | copy-start | bytes 1179652
  7.2 132.4 %copy-start.2 = (f32[1536]{0:T(1024)S(1)}, f32[1536]{0:T(1024)}, u32[]{:S(2)}) copy-start(f32[1536]{0:T(1024)} %param.16) | copy-start | bytes 18436
  7.2 185.7 %all-gather.3.cloned.1.call-start = ((), (), s32[]{:S(2)}) async-start(), calls=%async_computation.1 | async-start | bytes 1179648 | tf_op jit(solution)/shard_map/all_gather | solution.py:363
  16.3 127.1 %copy-start.6 = (s32[1,6]{1,0:T(1,128)S(1)}, s32[1,6]{1,0:T(1,128)}, u32[]{:S(2)}) copy-start(s32[1,6]{1,0:T(1,128)} %param.18) | copy-start | bytes 76
  145.6 121.5 %all-gather.5.cloned.1.call-start = ((), (), s32[]{:S(2)}) async-start(), calls=%async_computation.2 | async-start | bytes 3538944 | tf_op jit(solution)/shard_map/all_gather | solution.py:407
  202.7 3.3 copy-start.3
  202.7 4.2 %copy-start.5 = (bf16[128,4]{0,1:T(4,128)(2,1)S(1)}, bf16[128,4]{0,1:T(4,128)(2,1)}, u32[]{:S(2)}) copy-start(bf16[128,4]{0,1:T(4,128)(2,1)} %param.21) | copy-start | bytes 3076
  202.7 4.3 %copy-start.4 = (s32[128,4]{0,1:T(4,128)S(1)}, s32[128,4]{0,1:T(4,128)}, u32[]{:S(2)}) copy-start(s32[128,4]{0,1:T(4,128)} %param.20) | copy-start | bytes 6148
  206.9 155.7 %reduce-scatter.2.cloned.1.call-start = ((), (), s32[]{:S(2)}) async-start(), calls=%async_computation.3 | async-start | bytes 3538944 | tf_op jit(solution)/shard_map/reduce_scatter | solution.py:428
  269.9 8.1 %slice-start = ((s8[4718592]{0:T(1024)(128)(4,1)}), s8[4194304]{0:T(1024)(128)(4,1)S(1)}, s32[]{:S(2)}) async-start(s8[4718592]{0:T(1024)(128)(4,1)} %bitcast.102), calls=%async_computation.4 | async-start | bytes 8388608
  270.2 7.8 %slice-start.1 = ((s8[4718592]{0:T(1024)(128)(4,1)}), s8[524288]{0:T(1024)(128)(4,1)S(1)}, s32[]{:S(2)}) async-start(s8[4718592]{0:T(1024)(128)(4,1)} %bitcast.102), calls=%async_computation.5 | async-start | bytes 1048576
  280.8 2.7 copy-start.7
  280.8 4.1 %copy-start = (bf16[1024,512]{1,0:T(8,128)(2,1)S(1)}, bf16[1024,512]{1,0:T(8,128)(2,1)}, u32[]{:S(2)}) copy-start(bf16[1024,512]{1,0:T(8,128)(2,1)} %all-gather.3.cloned.1.call-done) | copy-start | bytes 3145732
Sparse Core Ops, SparseCore 0:
  145.7 47.1 all-gather.2
  207.0 59.9 all-gather.4
  283.7 78.8 reduce-scatter.1

commit v2 on v1

v2 whole, which is shorter than its diff:
```python
import math

import jax
import jax.numpy as jnp
from jax import lax
from jax.experimental import pallas as pl
from jax.experimental.pallas import tpu as pltpu
from jax.sharding import PartitionSpec as P

D = 1536
FF = 768
QH = 12
KVH = 2
HD = 128
E = 16
PAGE = 128
CAP = 64
QW = 1536
BF = jnp.bfloat16
F32 = jnp.float32
MESH = pl.DeviceIdType.MESH


class Net:
    def __init__(self, send_sems, recv_sems):
        rep, blk = lax.axis_index("rep"), lax.axis_index("blk")
        self.y, self.xl, self.c = rep // 4, (rep // 2) % 2, rep % 2
        self.z, self.xh = blk // 2, blk % 2
        self.x = self.xh * 2 + self.xl
        self.ss, self.rs, self.used = send_sems, recv_sems, 0

    def dev(self, y=0, x=0, z=0, c=0):
        yy = (self.y + y) % 4
        xx = (self.x + x) % 4
        zz = (self.z + z) % 4
        cc = (self.c + c) % 2
        return ((yy * 2 + xx % 2) * 2 + cc, zz * 2 + xx // 2)

    def xflip(self):
        return (((self.y * 2 + 1 - self.xl) * 2) + self.c, self.z * 2 + self.xh)

    def take(self, n=1):
        k = self.used
        self.used = k + n
        return k

    def make(self, src, dst, to, k):
        return pltpu.make_async_remote_copy(
            src_ref=src,
            dst_ref=dst,
            send_sem=self.ss.at[k],
            recv_sem=self.rs.at[k],
            device_id=to,
            device_id_type=MESH,
        )

    def send(self, ref, to):
        cp = self.make(ref, ref, to, self.take())
        cp.start()
        return cp


def enter(net):
    barrier = pltpu.get_barrier_semaphore()
    around = [net.dev(x=1), net.dev(x=3), net.dev(c=1)]
    around += [net.dev(y=k) for k in (1, 2, 3)]
    around += [net.dev(z=dz, x=dx) for dz in range(4) for dx in (0, 2) if dz or dx]
    for to in around:
        pl.semaphore_signal(barrier, inc=1, device_id=to, device_id_type=MESH)
    pl.semaphore_wait(barrier, len(around))


def scaled(values, gain):
    mean_sq = jnp.mean(values * values, axis=-1, keepdims=True)
    return (values * lax.rsqrt(mean_sq + 1e-06) * gain).astype(BF)


def stack(pieces):
    return jnp.concatenate([p.astype(F32) for p in pieces], axis=0).astype(BF)


def layer_kernel(
    qs,
    ms,
    es,
    os,
    wts,
    tokens,
    gain_a,
    gain_m,
    lengths,
    table,
    mixed,
    pages,
    wq,
    wm,
    wi,
    wo,
    q1,
    m1,
    e1,
    o1,
    wt,
    xn,
    qh,
    kv,
    at,
    hid,
    rows,
    oh,
    ga,
    msk,
    ch,
    act,
    res,
    pa,
    pb,
    ra,
    rb,
    rx,
    rz,
    ss,
    rs,
):
    net = Net(ss, rs)
    y, xl, c, z, xh = net.y, net.xl, net.c, net.z, net.xh
    blk = z * 2 + xh
    sent = []

    def send(ref, to, dst=None):
        cp = net.make(ref, ref if dst is None else dst, to, net.take())
        cp.start()
        sent.append(cp)
        return cp

    def blk_dev(b):
        return ((y * 2 + xl) * 2 + c, b)

    enter(net)
    half = z // 2
    slot = (z % 2) * 2 + xh
    first = {}
    for name, src, dst in (("q", qs, q1), ("m", ms, m1)):
        base = net.take(4)
        for k in range(4):
            zt = (z + k) % 4
            cp = pltpu.make_async_remote_copy(
                src_ref=src.at[zt],
                dst_ref=dst.at[slot],
                send_sem=ss.at[base + k],
                recv_sem=rs.at[base + slot],
                device_id=((y * 2 + xl) * 2 + c, zt * 2 + half),
                device_id_type=MESH,
            )
            first[name, k] = cp
            if k:
                cp.start()
                continue

            @pl.when(half != xh)
            def _(cp=cp):
                cp.start()

            @pl.when(half == xh)
            def _(src=src, dst=dst):
                dst[pl.ds(slot, 1)] = src[pl.ds(z, 1)]

    for name, src, dst, per in (("e", es, e1, 2), ("o", os, o1, 2), ("w", wts, wt, 1)):
        base = net.take(8)
        for k in range(1, 8):
            to = (blk + k) % 8
            part = src.at[pl.ds(2 * to, 2)] if per == 2 else src.at[to]
            cp = pltpu.make_async_remote_copy(
                src_ref=part,
                dst_ref=dst.at[blk],
                send_sem=ss.at[base + k],
                recv_sem=rs.at[base + k],
                device_id=blk_dev(to),
                device_id_type=MESH,
            )
            cp.start()
            first[name, k] = cp
        if per == 2:
            dst[pl.ds(blk, 1)] = src[pl.ds(2 * blk, 2)][None]
        else:
            dst[pl.ds(blk, 1)] = src[pl.ds(blk, 1)]

    tok = tokens[...].astype(F32)
    xn[...] = scaled(tok, gain_a[...])
    start_of = []
    total = jnp.int32(0)
    for i in range(6):
        start_of.append(total)
        total = total + lengths[0, i]

    def segment(index):
        seg = jnp.zeros_like(index)
        begin = jnp.zeros_like(index)
        for s in start_of[1:]:
            seg = seg + (index >= s).astype(jnp.int32)
            begin = jnp.where(index >= s, s, begin)
        return seg, begin

    low = jnp.maximum(blk - 4, 0)
    mine = lax.broadcasted_iota(jnp.int32, (128, 1), 0) + blk * 128
    my_seg, my_begin = segment(mine)
    key_at = lax.broadcasted_iota(jnp.int32, (1, 640), 1) + low * 128
    key_seg, _ = segment(key_at)
    msk[...] = jnp.where((my_seg == key_seg) & (key_at <= mine), 1.0, 0.0).astype(F32)
    lane = lax.broadcasted_iota(jnp.int32, (1, 128), 1)
    step = (lane % 64).astype(F32)
    frequency = jnp.exp(step * (-2.0 * math.log(10000.0) / 128))
    angle = (mine - my_begin).astype(F32) * frequency
    cosine = jnp.cos(angle)
    sine = jnp.where(lane < 64, -jnp.sin(angle), jnp.sin(angle))

    def wait_first(src, dst, base):
        for j in range(4):
            own = (z == 2 * xh + j // 2) & (xh == j % 2)

            @pl.when(jnp.logical_not(own))
            def _(j=j):
                net.make(src.at[0], dst.at[0], net.dev(c=1), base + j).wait_recv()

    wait_first(qs, q1, 0)
    block = stack([q1[j] for j in range(4)])
    ca = pl.ds(pl.multiple_of(z * 256, 256), 256)
    cb = pl.ds(pl.multiple_of(1024 + z * 256, 256), 256)
    cm = pl.ds(pl.multiple_of(z * 384, 128), 384)
    wq[y, xl, c, xh, :, ca] = block[:, :256]
    wq[y, xl, c, xh, :, cb] = block[:, 256:]
    wait_first(ms, m1, 4)
    wm[y, xl, c, xh, :, cm] = stack([m1[j] for j in range(4)])
    xs = (1, 3, 2)
    q2 = [send(wq.at[y, xl, c, xh, :, col], net.dev(x=k)) for k in xs for col in (ca, cb)]
    m2 = [send(wm.at[y, xl, c, xh, :, cm], net.dev(x=k)) for k in xs]

    for k in range(1, 8):
        first["w", k].wait_recv()
    upper = (
        lax.broadcasted_iota(jnp.int32, (128, 128), 0)
        <= lax.broadcasted_iota(jnp.int32, (128, 128), 1)
    )
    upper = jnp.where(upper, 1.0, 0.0).astype(BF)
    slots = lax.broadcasted_iota(jnp.int32, (64, 128), 0).astype(F32)

    def tables(s, carry):
        w = wt[s]
        member = jnp.where(w > 0, 1.0, 0.0)
        rank = jnp.dot(member.astype(BF), upper, preferred_element_type=F32) - 1.0
        for e in range(2):
            hit = (member[e : e + 1] > 0) & (rank[e : e + 1] == slots)
            oh[s, e * 64 : e * 64 + 64] = jnp.where(hit, 1.0, 0.0).astype(BF)
            ga[s, e * 64 : e * 64 + 64] = jnp.where(hit, w[e : e + 1], 0.0).astype(BF)
        return carry

    lax.fori_loop(0, 8, tables, 0)

    for cp in q2:
        cp.wait_recv()
    q3a = [send(wq.at[y, :, c, :, :, ca], net.dev(y=k)) for k in xs]
    q3b = [send(wq.at[y, :, c, :, :, cb], net.dev(z=k)) for k in xs]
    for cp in m2:
        cp.wait_recv()
    m3 = [send(wm.at[y, :, c, :, :, cm], net.dev(y=k)) for k in xs]
    for cp in q3a:
        cp.wait_recv()
    q4a = [send(wq.at[:, :, c, :, :, ca], net.dev(z=k)) for k in xs]
    for cp in q3b:
        cp.wait_recv()
    cbb = pl.ds(1024, 1024)
    q4b = [send(wq.at[y, :, c, :, :, cbb], net.dev(y=k)) for k in xs]
    q5 = [
        send(wq.at[:, :, c, :, :, ca], net.dev(c=1)),
        send(wq.at[y, :, c, :, :, cbb], net.dev(c=1)),
    ]
    for k in range(1, 8):
        first["e", k].wait_recv()

    def lay(src, dst, width):
        def one(i, carry):
            col = pl.ds(pl.multiple_of(i * width, width), width)
            for e in range(2):
                dst[e, y, xl, c, :, col] = stack([src[j, e, :, col] for j in range(8)])
            return carry

        lax.fori_loop(0, D // width, one, 0)

    lay(e1, wi, 256)
    i1 = send(wi.at[:, y, xl, c], net.xflip())
    i2 = {k: send(wi.at[:, y, xl, c], net.dev(y=k)) for k in (1, 3)}
    for k in range(1, 8):
        first["o", k].wait_recv()
    lay(o1, wo, 256)
    u1 = {k: send(wo.at[:, y, xl, c], net.dev(y=k)) for k in xs}
    p5 = [send(wi.at[:, y, xl, c], net.dev(c=1)), send(wo.at[:, y, xl, c], net.dev(c=1))]
    u2 = [send(wo.at[:, y, xl, c], net.xflip())]
    for cp in m3:
        cp.wait_recv()
    m4 = [send(wm.at[:, :, c, :, :, cm], net.dev(z=k)) for k in xs]
    m5 = [send(wm.at[:, :, c, :, :, cm], net.dev(c=1))]
    i1.wait_recv()
    i3 = {k: send(wi.at[:, y, 1 - xl, c], net.dev(y=k)) for k in (1, 3)}
    p5 += [send(wi.at[:, y, 1 - xl, c], net.dev(c=1))]
    for n, k in enumerate(xs):
        q4a[n].wait_recv()
        zf = (z + 4 - k) % 4
        col = pl.ds(pl.multiple_of(zf * 256, 256), 256)
        q5.append(send(wq.at[:, :, c, :, :, col], net.dev(c=1)))
        q4b[n].wait_recv()
        q5.append(send(wq.at[(y + 4 - k) % 4, :, c, :, :, cbb], net.dev(c=1)))
    for cp in q5:
        cp.wait_recv()

    def project(col):
        w = wq[:, :, :, :, :, col].reshape(D, 256)
        return jnp.dot(xn[...], w, preferred_element_type=F32)

    def turned(head):
        return (head * cosine + pltpu.roll(head, 64, 1) * sine).astype(BF)

    kk = project(pl.ds(1536, 256))
    vv = project(pl.ds(1792, 256))
    kv[pl.ds(blk, 1), :, pl.ds(0, 128)] = turned(kk[:, :128])[None]
    kv[pl.ds(blk, 1), :, pl.ds(128, 128)] = turned(kk[:, 128:])[None]
    kv[pl.ds(blk, 1), :, pl.ds(256, 256)] = vv.astype(BF)[None]
    kvs = [send(kv.at[blk], blk_dev((blk + k) % 8)) for k in range(1, 8)]

    def query(n, carry):
        p = project(pl.ds(pl.multiple_of(n * 256, 256), 256))
        qh[pl.ds(2 * n, 1)] = turned(p[:, :128])[None]
        qh[pl.ds(2 * n + 1, 1)] = turned(p[:, 128:])[None]
        return carry

    lax.fori_loop(0, 6, query, 0)
    up, down = net.dev(y=1), net.dev(y=3)
    lo, hi = (y + 3) % 4, (y + 1) % 4
    for cp in kvs:
        cp.wait_recv()
    pages[...] = kv[table[0, 0]]

    def attend(h, carry):
        g = h // 6
        k = kv[pl.ds(low, 5), :, pl.ds(pl.multiple_of(g * 128, 128), 128)].reshape(640, 128)
        v = kv[pl.ds(low, 5), :, pl.ds(pl.multiple_of(256 + g * 128, 128), 128)].reshape(640, 128)
        s = lax.dot_general(qh[h], k, (((1,), (1,)), ((), ())), preferred_element_type=F32)
        s = jnp.where(msk[...] > 0, s * (1.0 / math.sqrt(HD)), -1e30)
        w = jnp.exp(s - jnp.max(s, axis=-1, keepdims=True))
        p = (w / jnp.sum(w, axis=-1, keepdims=True)).astype(BF)
        a = jnp.dot(p, v, preferred_element_type=F32)
        at[:, pl.ds(pl.multiple_of(h * 128, 128), 128)] = a.astype(BF)
        return carry

    lax.fori_loop(0, 12, attend, 0)
    for n, k in enumerate(xs):
        m4[n].wait_recv()
        zf = (z + 4 - k) % 4
        col = pl.ds(pl.multiple_of(zf * 384, 128), 384)
        m5.append(send(wm.at[:, :, c, :, :, col], net.dev(c=1)))
    for k in (1, 3):
        i2[k].wait_recv()
    for k in (1, 3):
        i3[k].wait_recv()
    r4 = [send(wi.at[:, lo, 0, c], up), send(wi.at[:, hi, 1, c], down)]
    p6 = [send(wi.at[:, lo, :, c], net.dev(c=1)), send(wi.at[:, hi, :, c], net.dev(c=1))]
    for cp in m5:
        cp.wait_recv()

    def mix(n, carry):
        col = pl.ds(pl.multiple_of(n * 256, 256), 256)
        w = wm[:, :, :, :, :, col].reshape(D, 256)
        hid[:, col] = tokens[:, col].astype(F32) + jnp.dot(
            at[...], w, preferred_element_type=F32
        )
        return carry

    lax.fori_loop(0, 6, mix, 0)
    rows[pl.ds(blk, 1)] = scaled(hid[...], gain_m[...])[None]
    across = net.dev(x=2)
    t1 = {k: send(rows.at[blk], net.dev(z=k)) for k in xs}
    tx = send(rows.at[blk], across)

    for k in xs:
        u1[k].wait_recv()
        yf = (y + 4 - k) % 4
        u2.append(send(wo.at[:, yf, xl, c], net.xflip()))
        p6.append(send(wo.at[:, yf, xl, c], net.dev(c=1)))
    for n, k in enumerate((0,) + xs):
        u2[n].wait_recv()
        p6.append(send(wo.at[:, (y + 4 - k) % 4, 1 - xl, c], net.dev(c=1)))
    for cp in r4:
        cp.wait_recv()
    p6.append(send(wi.at[:, (y + 2) % 4, :, c], net.dev(c=1)))
    tx.wait_recv()
    blk_x = z * 2 + 1 - xh
    t2 = {k: send(rows.at[blk_x], net.dev(z=k)) for k in (1, 3)}
    t1[2].wait_recv()
    blk_o = ((z + 2) % 4) * 2 + xh
    t3 = send(rows.at[blk_o], across)
    for k in (1, 3):
        t1[k].wait_recv()
    for cp in p5 + p6:
        cp.wait_recv()

    order = (0, 1, 3, 2)

    def experts(plane, out):
        for j, dz in enumerate(order):
            s = ((z + dz) % 4) * 2 + plane

            def pick(n, carry, s=s, j=j):
                col = pl.ds(pl.multiple_of(n * 512, 512), 512)
                got = jnp.dot(oh[s], rows[s, :, col], preferred_element_type=F32).astype(BF)
                ch[0, j * 64 : j * 64 + 64, col] = got[:64]
                ch[1, j * 64 : j * 64 + 64, col] = got[64:]
                return carry

            lax.fori_loop(0, 3, pick, 0)

        def one(e, carry):
            def gate(n, carry):
                lo_col = pl.ds(pl.multiple_of(n * 256, 256), 256)
                up_col = pl.ds(pl.multiple_of(768 + n * 256, 256), 256)
                a = jnp.dot(
                    ch[e], wi[e, :, :, :, :, lo_col].reshape(D, 256), preferred_element_type=F32
                )
                b = jnp.dot(
                    ch[e], wi[e, :, :, :, :, up_col].reshape(D, 256), preferred_element_type=F32
                )
                act[:, lo_col] = (jnp.maximum(a, 0.0) * b).astype(BF)
                return carry

            lax.fori_loop(0, 3, gate, 0)

            def down_to(n, carry):
                col = pl.ds(pl.multiple_of(n * 256, 256), 256)
                r = jnp.dot(
                    act[...], wo[e, :, :, :, :, col].reshape(FF, 256), preferred_element_type=F32
                ).astype(BF)
                for j in range(4):
                    res[j, pl.ds(pl.multiple_of(e * 64, 64), 64), col] = r[j * 64 : j * 64 + 64]
                return carry

            lax.fori_loop(0, 6, down_to, 0)
            return carry

        lax.fori_loop(0, 2, one, 0)
        for j, dz in enumerate(order):
            s = ((z + dz) % 4) * 2 + plane

            def fold(n, carry, s=s, j=j, dz=dz):
                col = pl.ds(pl.multiple_of(n * 512, 512), 512)
                t = lax.dot_general(
                    ga[s], res[j, :, col], (((0,), (0,)), ((), ())), preferred_element_type=F32
                )
                if out is pa and dz == 0:
                    hid[:, col] = hid[:, col] + t
                else:
                    out[dz, :, col] = t.astype(BF)
                return carry

            lax.fori_loop(0, 3, fold, 0)

    experts(xh, pa)
    s1 = [send(pa.at[k], net.dev(z=k), ra.at[k // 2]) for k in (1, 3)]
    for cp in t2.values():
        cp.wait_recv()
    t3.wait_recv()
    experts(1 - xh, pb)
    s2 = [send(pb.at[2], across, rx.at[0])]
    s3 = [send(pb.at[k], net.dev(z=k), rb.at[k // 2]) for k in (1, 3)]
    for cp in s1:
        cp.wait_recv()
    hid[...] = hid[...] + ra[0].astype(F32) + ra[1].astype(F32)
    s2[0].wait_recv()
    pa[2] = (pa[2].astype(F32) + rx[0].astype(F32)).astype(BF)
    s4 = send(pa.at[2], net.dev(z=2), rz)
    for cp in s3:
        cp.wait_recv()
    pb[0] = (pb[0].astype(F32) + rb[0].astype(F32) + rb[1].astype(F32)).astype(BF)
    s5 = send(pb.at[0], across, rx.at[1])
    s4.wait_recv()
    s5.wait_recv()
    mixed[...] = (hid[...] + rz[...].astype(F32) + rx[1].astype(F32)).astype(BF)
    for (name, k), cp in first.items():
        if k:
            cp.wait_send()
        else:

            @pl.when(half != xh)
            def _(cp=cp):
                cp.wait_send()

    for cp in sent:
        cp.wait_send()


def layer_call(*args):
    vm = pl.BlockSpec(memory_space=pltpu.VMEM)
    sm = pl.BlockSpec(memory_space=pltpu.SMEM)
    return pl.pallas_call(
        layer_kernel,
        out_shape=(
            jax.ShapeDtypeStruct((128, D), BF),
            jax.ShapeDtypeStruct((128, 512), BF),
        ),
        in_specs=[vm] * 8 + [sm] * 2,
        out_specs=(vm,) * 2,
        scratch_shapes=[
            pltpu.VMEM((4, 2, 2, 2, 48, 2048), BF),
            pltpu.VMEM((4, 2, 2, 2, 48, D), BF),
            pltpu.VMEM((2, 4, 2, 2, 96, D), BF),
            pltpu.VMEM((2, 4, 2, 2, 48, D), BF),
            pltpu.VMEM((4, 12, 512), BF),
            pltpu.VMEM((4, 12, 384), BF),
            pltpu.VMEM((8, 2, 12, D), BF),
            pltpu.VMEM((8, 2, 6, D), BF),
            pltpu.VMEM((8, 2, 128), F32),
            pltpu.VMEM((128, D), BF),
            pltpu.VMEM((12, 128, 128), BF),
            pltpu.VMEM((8, 128, 512), BF),
            pltpu.VMEM((128, D), BF),
            pltpu.VMEM((128, D), F32),
            pltpu.VMEM((8, 128, D), BF),
            pltpu.VMEM((8, 128, 128), BF),
            pltpu.VMEM((8, 128, 128), BF),
            pltpu.VMEM((128, 640), F32),
            pltpu.VMEM((2, 256, D), BF),
            pltpu.VMEM((256, FF), BF),
            pltpu.VMEM((4, 128, D), BF),
            pltpu.VMEM((4, 128, D), BF),
            pltpu.VMEM((4, 128, D), BF),
            pltpu.VMEM((2, 128, D), BF),
            pltpu.VMEM((2, 128, D), BF),
            pltpu.VMEM((2, 128, D), BF),
            pltpu.VMEM((128, D), BF),
            pltpu.SemaphoreType.DMA((160,)),
            pltpu.SemaphoreType.DMA((160,)),
        ],
        compiler_params=pltpu.CompilerParams(
            collective_id=0, has_side_effects=True, vmem_limit_bytes=64 << 20
        ),
    )(*args)


def body(
    tokens,
    attn_in,
    attn_out,
    expert_in,
    expert_out,
    attn_gain,
    moe_gain,
    lengths,
    page_table,
    routes,
    gates,
):
    place = lax.axis_index("blk")
    qs = attn_in.astype(BF).reshape(12, 2, 4, 256).transpose(2, 0, 1, 3).reshape(4, 12, 512)
    ms = attn_out.astype(BF).reshape(12, 4, 384).transpose(1, 0, 2)
    ids = jnp.arange(E, dtype=jnp.int32)
    weight = jnp.sum(
        jnp.where(
            routes.T[None, :, :] == ids[:, None, None], gates.astype(F32).T[None, :, :], 0.0
        ),
        axis=1,
    ).reshape(8, 2, 128)
    page_ids = jnp.arange(8, dtype=jnp.int32)
    logical = jnp.sum(jnp.where(page_table == place, page_ids[None, :], 0), axis=1, keepdims=True)
    mixed, pages = layer_call(
        qs,
        ms,
        expert_in.astype(BF),
        expert_out.astype(BF),
        weight,
        tokens,
        attn_gain[None],
        moe_gain[None],
        lengths,
        logical,
    )
    return mixed, pages[None]


def solution(mesh):
    in_specs = (
        P(("rep", "blk"), None),
        P(("rep", "blk"), None),
        P(("rep", "blk"), None),
        P(None, ("rep", "blk"), None),
        P(None, ("rep", "blk"), None),
        P(),
        P(),
        P("rep", None),
        P("rep", None),
        P(("rep", "blk"), None),
        P(("rep", "blk"), None),
    )
    out_specs = (P(("rep", "blk"), None), P(("rep", "blk"), None, None))
    return jax.shard_map(body, mesh=mesh, in_specs=in_specs, out_specs=out_specs, check_vma=False)
```

time: 373 us -> 193 us (0.52)
  waiting for transfers between devices: 130 us -> 0 us
  Pallas kernels: 123 us -> 182 us
  other arithmetic: 34.3 us -> 2.69 us
  matrix products: 31.4 us -> 0 us
  blocking collectives: 28.5 us -> 0 us
  between operations: 14.9 us -> 0.73 us
    reduce_scatter x1 -> x0, waiting for transfers between devices: 76.2 us -> none  [body(): lax.psum_scatter(summed.reshape(count * lax.axis_size('blk'), D).astype(j...]
    pallas_call x1, Pallas kernels: 123 us -> 182 us  [layer_call(): pl.pallas_call(layer_kernel, out_shape=(jax.ShapeDtypeStruct((128, D), BF...]
    all_gather x2 -> x0, waiting for transfers between devices: 53.6 us -> none  [the longest x1 46 us: body(): cache_all = lax.all_gather(cache_here, 'blk', axis=0, tiled=True)]
    all_gather x1 -> x0, blocking collectives: 28.5 us -> none  [body(): lax.all_gather(dense, 'blk', axis=0, tiled=True)]
    dot_general x7 -> x0, matrix products: 26.6 us -> none  [the longest x1 7.76 us: body(): jnp.einsum('erd,edf->erf', section, wi, preferred_element_type=jnp.float32)]
    another operation x4 -> x0, other arithmetic: 24 us -> none  [the longest x1 23.4 us: slot_tables(): ranked = jnp.cumsum(member, axis=0) - 1]
    sub x1 -> x0, matrix products: 4.83 us -> none  [body(): weights = jnp.exp(scores - highest)]
  transfers between devices with their start and end apart: 3 -> 0, of which waited for: 3 -> 0; matrix products, arithmetic and copies ran while one was open for 7% -> 0% of each run, Pallas kernels for 0% -> 0%
where the time goes in v2:
time: 193 us
  Pallas kernels  182 us (94%)
  local copies, waits for them, and re-layouts  8.11 us (4%)
  other arithmetic  2.69 us (1%)
    pallas_call x1, Pallas kernels, layer_call(): pl.pallas_call(layer_kernel, out_shape=(jax.ShapeDtypeStruct((128, D), BF...  182 us

profile of v2, /device:TPU:96, one launch (start us, length us, event | category | flops | bytes accessed | tf_op | source)
XLA Modules:
  0.0 193.1 jit_solution(5646545447302703126)
XLA Ops:
  0.6 0.0 copy-start
  0.6 1.4 convert_element_type.15
  2.0 0.0 copy-start.1
  2.1 1.2 copy.29.es
  3.3 0.0 copy-done
  3.3 0.0 copy-start.2
  3.3 0.0 copy-start.6
  3.3 0.0 copy-start.5
  3.3 0.0 copy-start.3
  3.3 0.0 copy-start.4
  3.3 0.0 copy-start.7
  3.4 0.9 copy.30.os
  4.3 0.0 copy-done.1
  4.4 0.6 copy.28.qs
  5.1 0.0 copy-done.2
  5.1 0.6 copy.33
  5.7 0.0 copy-done.6
  5.7 0.0 copy-done.5
  5.7 0.6 select_reduce_fusion
  6.3 0.0 copy-done.3
  6.3 0.6 broadcast_in_dim.34.gain_a
  6.9 0.0 copy-done.4
  6.9 0.6 broadcast_in_dim.35.gain_m
  7.5 0.0 copy-done.7
  7.5 0.6 fusion
  8.2 181.6 %shard_map.122 = (bf16[128,1536]{1,0:T(8,128)(2,1)}, bf16[128,512]{1,0:T(8,128)(2,1)}) custom-call(bf16[4,12,512]{2,1,0:T(8,128)(2,1)} %copy.28.qs, bf16[4,12,384]{2,1,0:T(8,128)(2,1)} %bitcast.14, bf16[16,12,1536]{2,1,0:T(8,128)(2,1)} %copy.29.es, bf16[16,6,1536]{2,1,0:T(8,128)(2,1)} %copy.30.os, f32[8,2,128]{2,1,0:T(2,128)} %bitcast.17, ...), custom_call_target="tpu_custom_call" | custom-call | tf_op jit(solution)/shard_map/pallas_call | solution.py:501
  189.8 1.8 copy.37
  191.5 1.6 copy.38
  (8 shorter events, 0.2 us)
Async XLA Ops:
  0.6 2.7 %copy-start = (f32[16,6,1536]{2,0,1:T(8,128)S(1)}, f32[16,6,1536]{2,0,1:T(8,128)}, u32[]{:S(2)}) copy-start(f32[16,6,1536]{2,0,1:T(8,128)} %param.15) | copy-start | bytes 1769476
  2.0 2.2 %copy-start.1 = (f32[12,2048]{1,0:T(8,128)S(1)}, f32[12,2048]{1,0:T(8,128)}, u32[]{:S(2)}) copy-start(f32[12,2048]{1,0:T(8,128)} %param.12) | copy-start | bytes 294916
  3.3 1.8 copy-start.2
  3.3 2.5 %copy-start.6 = (bf16[128,4]{0,1:T(4,128)(2,1)S(1)}, bf16[128,4]{0,1:T(4,128)(2,1)}, u32[]{:S(2)}) copy-start(bf16[128,4]{0,1:T(4,128)(2,1)} %param.21) | copy-start | bytes 3076
  3.3 2.5 %copy-start.5 = (s32[128,4]{0,1:T(4,128)S(1)}, s32[128,4]{0,1:T(4,128)}, u32[]{:S(2)}) copy-start(s32[128,4]{0,1:T(4,128)} %param.20) | copy-start | bytes 6148
  3.3 3.0 %copy-start.3 = (f32[1536]{0:T(1024)S(1)}, f32[1536]{0:T(1024)}, u32[]{:S(2)}) copy-start(f32[1536]{0:T(1024)} %param.16) | copy-start | bytes 18436
  3.3 3.6 %copy-start.4 = (f32[1536]{0:T(1024)S(1)}, f32[1536]{0:T(1024)}, u32[]{:S(2)}) copy-start(f32[1536]{0:T(1024)} %param.17) | copy-start | bytes 18436
  3.3 4.2 %copy-start.7 = (s32[1,8]{1,0:T(1,128)S(1)}, s32[1,8]{1,0:T(1,128)}, u32[]{:S(2)}) copy-start(s32[1,8]{1,0:T(1,128)} %param.19) | copy-start | bytes 100

commit v3 on v2

--- a/solution.py
+++ b/solution.py
@@ -80,12 +80,12 @@
 
 
 def layer_kernel(
-    qs,
-    ms,
-    es,
-    os,
+    xq,
+    xm,
+    xe,
+    xo,
+    tokens,
     wts,
-    tokens,
     gain_a,
     gain_m,
     lengths,
@@ -96,6 +96,15 @@
     wm,
     wi,
     wo,
+    fq,
+    fm,
+    fe,
+    fo,
+    tk,
+    qs,
+    ms,
+    es,
+    os,
     q1,
     m1,
     e1,
@@ -104,6 +113,7 @@
     xn,
     qh,
     kv,
+    near,
     at,
     hid,
     rows,
@@ -119,6 +129,7 @@
     rb,
     rx,
     rz,
+    ls,
     ss,
     rs,
 ):
@@ -136,6 +147,22 @@
     def blk_dev(b):
         return ((y * 2 + xl) * 2 + c, b)
 
+    loads = []
+    for n, (src, dst) in enumerate(
+        ((xq, fq), (xm, fm), (tokens, tk), (xe, fe), (xo, fo))
+    ):
+        cp = pltpu.make_async_copy(src, dst, ls.at[n])
+        cp.start()
+        loads.append(cp)
+    loads[0].wait()
+    for k in range(4):
+        qs[k, :, 0:128] = fq[:, k * 128 : k * 128 + 128].astype(BF)
+        qs[k, :, 128:384] = fq[:, 512 + k * 256 : 768 + k * 256].astype(BF)
+        qs[k, :, 384:512] = fq[:, 1536 + k * 128 : 1664 + k * 128].astype(BF)
+    loads[1].wait()
+    for k in range(4):
+        ms[k, :, 0:128] = fm[:, k * 128 : k * 128 + 128].astype(BF)
+        ms[k, :, 128:384] = fm[:, 512 + k * 256 : 768 + k * 256].astype(BF)
     enter(net)
     half = z // 2
     slot = (z % 2) * 2 + xh
@@ -165,13 +192,12 @@
             def _(src=src, dst=dst):
                 dst[pl.ds(slot, 1)] = src[pl.ds(z, 1)]
 
-    for name, src, dst, per in (("e", es, e1, 2), ("o", os, o1, 2), ("w", wts, wt, 1)):
+    def spread(name, src, dst):
         base = net.take(8)
         for k in range(1, 8):
             to = (blk + k) % 8
-            part = src.at[pl.ds(2 * to, 2)] if per == 2 else src.at[to]
             cp = pltpu.make_async_remote_copy(
-                src_ref=part,
+                src_ref=src.at[to],
                 dst_ref=dst.at[blk],
                 send_sem=ss.at[base + k],
                 recv_sem=rs.at[base + k],
@@ -180,13 +206,12 @@
             )
             cp.start()
             first[name, k] = cp
-        if per == 2:
-            dst[pl.ds(blk, 1)] = src[pl.ds(2 * blk, 2)][None]
-        else:
-            dst[pl.ds(blk, 1)] = src[pl.ds(blk, 1)]
-
-    tok = tokens[...].astype(F32)
-    xn[...] = scaled(tok, gain_a[...])
+        dst[pl.ds(blk, 1)] = src[pl.ds(blk, 1)]
+
+    spread("w", wts, wt)
+    loads[2].wait()
+    tok = tk[...].astype(F32)
+    xn[...] = scaled(tok, gain_a[...].reshape(1, D))
     start_of = []
     total = jnp.int32(0)
     for i in range(6):
@@ -201,40 +226,109 @@
             begin = jnp.where(index >= s, s, begin)
         return seg, begin
 
-    low = jnp.maximum(blk - 4, 0)
+    low = blk - 4
+    for k in range(1, 5):
+
+        @pl.when(blk < k)
+        def _(k=k):
+            near[4 - k] = jnp.zeros((128, 512), BF)
+
     mine = lax.broadcasted_iota(jnp.int32, (128, 1), 0) + blk * 128
     my_seg, my_begin = segment(mine)
+
+    def wait_first(src, dst, base):
+        for j in range(4):
+            own = (z == 2 * xh + j // 2) & (xh == j % 2)
+
+            @pl.when(jnp.logical_not(own))
+            def _(j=j):
+                net.make(src.at[0], dst.at[0], net.dev(c=1), base + j).wait_recv()
+
+    def zcol(base, width, at):
+        return pl.ds(pl.multiple_of(base + at * width, 128), width)
+
+    xs = (1, 3, 2)
+
+    class Color:
+        def __init__(self, ref, base, width, axes):
+            self.ref, self.base, self.width, self.axes = ref, base, width, axes
+            self.stage, self.chip = 0, []
+
+        def view(self, axes, **moved):
+            at = {"y": y, "x": net.x, "z": z, **moved}
+            yy = slice(None) if "y" in axes else at["y"]
+            xx = slice(None) if "x" in axes else at["x"] % 2
+            hh = slice(None) if "x" in axes else at["x"] // 2
+            whole = pl.ds(self.base, 4 * self.width)
+            cc = whole if "z" in axes else zcol(self.base, self.width, at["z"])
+            return self.ref.at[yy, xx, c, hh, :, cc]
+
+        def go(self):
+            axis, done = self.axes[self.stage], self.axes[: self.stage]
+            part = self.view(done)
+            self.cps = [send(part, net.dev(**{axis: k})) for k in xs]
+            self.stage += 1
+            if self.stage == 3:
+                self.chip.append(send(part, net.dev(c=1)))
+
+        def arrive(self):
+            for cp in self.cps:
+                cp.wait_recv()
+
+        def land(self, n):
+            axis = self.axes[2]
+            self.cps[n].wait_recv()
+            here = {"y": y, "x": net.x, "z": z}[axis]
+            got = self.view(self.axes[:2], **{axis: (here + 4 - xs[n]) % 4})
+            self.chip.append(send(got, net.dev(c=1)))
+
+        def close(self):
+            for cp in self.chip:
+                cp.wait_recv()
+
+    qc = [Color(wq, 512, 256, "xzy"), Color(wq, 0, 128, "xyz"), Color(wq, 1536, 128, "yzx")]
+    mc = [Color(wm, 512, 256, "yzx"), Color(wm, 0, 128, "xyz")]
+    wait_first(qs, q1, 0)
+    block = stack([q1[j] for j in range(4)])
+    wq[y, xl, c, xh, :, zcol(0, 128, z)] = block[:, 0:128]
+    wq[y, xl, c, xh, :, zcol(512, 256, z)] = block[:, 128:384]
+    wq[y, xl, c, xh, :, zcol(1536, 128, z)] = block[:, 384:512]
+    for q in qc:
+        q.go()
+    wait_first(ms, m1, 4)
+    block = stack([m1[j] for j in range(4)])
+    wm[y, xl, c, xh, :, zcol(0, 128, z)] = block[:, 0:128]
+    wm[y, xl, c, xh, :, zcol(512, 256, z)] = block[:, 128:384]
+    for m in mc:
+        m.go()
+    loads[3].wait()
+    loads[4].wait()
+
+    for d in range(8):
+        es[d] = stack([fe[:, 2 * d], fe[:, 2 * d + 1]])
+        os[d] = stack(
+            [fo[:, 2 * d + i // 2, i % 2 * 768 : i % 2 * 768 + 768] for i in range(4)]
+        )
+    for q in qc:
+        q.arrive()
+        q.go()
+    spread("e", es, e1)
+    spread("o", os, o1)
     key_at = lax.broadcasted_iota(jnp.int32, (1, 640), 1) + low * 128
     key_seg, _ = segment(key_at)
-    msk[...] = jnp.where((my_seg == key_seg) & (key_at <= mine), 1.0, 0.0).astype(F32)
+    msk[...] = jnp.where((my_seg == key_seg) & (key_at <= mine) & (key_at >= 0), 1.0, 0.0).astype(F32)
     lane = lax.broadcasted_iota(jnp.int32, (1, 128), 1)
     step = (lane % 64).astype(F32)
     frequency = jnp.exp(step * (-2.0 * math.log(10000.0) / 128))
     angle = (mine - my_begin).astype(F32) * frequency
     cosine = jnp.cos(angle)
     sine = jnp.where(lane < 64, -jnp.sin(angle), jnp.sin(angle))
-
-    def wait_first(src, dst, base):
-        for j in range(4):
-            own = (z == 2 * xh + j // 2) & (xh == j % 2)
-
-            @pl.when(jnp.logical_not(own))
-            def _(j=j):
-                net.make(src.at[0], dst.at[0], net.dev(c=1), base + j).wait_recv()
-
-    wait_first(qs, q1, 0)
-    block = stack([q1[j] for j in range(4)])
-    ca = pl.ds(pl.multiple_of(z * 256, 256), 256)
-    cb = pl.ds(pl.multiple_of(1024 + z * 256, 256), 256)
-    cm = pl.ds(pl.multiple_of(z * 384, 128), 384)
-    wq[y, xl, c, xh, :, ca] = block[:, :256]
-    wq[y, xl, c, xh, :, cb] = block[:, 256:]
-    wait_first(ms, m1, 4)
-    wm[y, xl, c, xh, :, cm] = stack([m1[j] for j in range(4)])
-    xs = (1, 3, 2)
-    q2 = [send(wq.at[y, xl, c, xh, :, col], net.dev(x=k)) for k in xs for col in (ca, cb)]
-    m2 = [send(wm.at[y, xl, c, xh, :, cm], net.dev(x=k)) for k in xs]
-
+    for q in qc:
+        q.arrive()
+        q.go()
+    for m in mc:
+        m.arrive()
+        m.go()
     for k in range(1, 8):
         first["w", k].wait_recv()
     upper = (
@@ -255,62 +349,44 @@
         return carry
 
     lax.fori_loop(0, 8, tables, 0)
-
-    for cp in q2:
-        cp.wait_recv()
-    q3a = [send(wq.at[y, :, c, :, :, ca], net.dev(y=k)) for k in xs]
-    q3b = [send(wq.at[y, :, c, :, :, cb], net.dev(z=k)) for k in xs]
-    for cp in m2:
-        cp.wait_recv()
-    m3 = [send(wm.at[y, :, c, :, :, cm], net.dev(y=k)) for k in xs]
-    for cp in q3a:
-        cp.wait_recv()
-    q4a = [send(wq.at[:, :, c, :, :, ca], net.dev(z=k)) for k in xs]
-    for cp in q3b:
-        cp.wait_recv()
-    cbb = pl.ds(1024, 1024)
-    q4b = [send(wq.at[y, :, c, :, :, cbb], net.dev(y=k)) for k in xs]
-    q5 = [
-        send(wq.at[:, :, c, :, :, ca], net.dev(c=1)),
-        send(wq.at[y, :, c, :, :, cbb], net.dev(c=1)),
-    ]
     for k in range(1, 8):
         first["e", k].wait_recv()
 
-    def lay(src, dst, width):
-        def one(i, carry):
-            col = pl.ds(pl.multiple_of(i * width, width), width)
-            for e in range(2):
-                dst[e, y, xl, c, :, col] = stack([src[j, e, :, col] for j in range(8)])
-            return carry
-
-        lax.fori_loop(0, D // width, one, 0)
-
-    lay(e1, wi, 256)
-    i1 = send(wi.at[:, y, xl, c], net.xflip())
-    i2 = {k: send(wi.at[:, y, xl, c], net.dev(y=k)) for k in (1, 3)}
+    def lay_in(i, carry):
+        col = pl.ds(pl.multiple_of(i * 256, 256), 256)
+        got = [e1[j, :, col].astype(F32) for j in range(8)]
+        for e in range(2):
+            part = [g[e * 12 : e * 12 + 12] for g in got]
+            wi[e, y, xl, c, :, col] = jnp.concatenate(part, axis=0).astype(BF)
+        return carry
+
+    def lay_out(i, carry):
+        col = pl.ds(pl.multiple_of(i * 256, 256), 256)
+        got = [o1[j, :, col].astype(F32) for j in range(8)]
+        for n in range(4):
+            part = [g[n * 6 : n * 6 + 6] for g in got]
+            to = pl.ds(pl.multiple_of(n % 2 * 768 + i * 256, 256), 256)
+            wo[n // 2, y, xl, c, :, to] = jnp.concatenate(part, axis=0).astype(BF)
+        return carry
+
+    lax.fori_loop(0, 6, lay_in, 0)
+    i1 = [send(wi.at[:, y, xl, c], net.xflip())]
+    i2 = {k: [send(wi.at[:, y, xl, c], net.dev(y=k))] for k in (1, 3)}
     for k in range(1, 8):
         first["o", k].wait_recv()
-    lay(o1, wo, 256)
-    u1 = {k: send(wo.at[:, y, xl, c], net.dev(y=k)) for k in xs}
-    p5 = [send(wi.at[:, y, xl, c], net.dev(c=1)), send(wo.at[:, y, xl, c], net.dev(c=1))]
-    u2 = [send(wo.at[:, y, xl, c], net.xflip())]
-    for cp in m3:
-        cp.wait_recv()
-    m4 = [send(wm.at[:, :, c, :, :, cm], net.dev(z=k)) for k in xs]
-    m5 = [send(wm.at[:, :, c, :, :, cm], net.dev(c=1))]
-    i1.wait_recv()
-    i3 = {k: send(wi.at[:, y, 1 - xl, c], net.dev(y=k)) for k in (1, 3)}
-    p5 += [send(wi.at[:, y, 1 - xl, c], net.dev(c=1))]
-    for n, k in enumerate(xs):
-        q4a[n].wait_recv()
-        zf = (z + 4 - k) % 4
-        col = pl.ds(pl.multiple_of(zf * 256, 256), 256)
-        q5.append(send(wq.at[:, :, c, :, :, col], net.dev(c=1)))
-        q4b[n].wait_recv()
-        q5.append(send(wq.at[(y + 4 - k) % 4, :, c, :, :, cbb], net.dev(c=1)))
-    for cp in q5:
-        cp.wait_recv()
+    lax.fori_loop(0, 3, lay_out, 0)
+    i1.append(send(wo.at[:, y, xl, c], net.xflip()))
+    for k in (1, 3):
+        i2[k].append(send(wo.at[:, y, xl, c], net.dev(y=k)))
+    for m in mc:
+        m.arrive()
+        m.go()
+    for n in range(3):
+        for q in qc:
+            q.land(n)
+    p5 = [send(w.at[:, y, xl, c], net.dev(c=1)) for w in (wi, wo)]
+    for q in qc:
+        q.close()
 
     def project(col):
         w = wq[:, :, :, :, :, col].reshape(D, 256)
@@ -321,10 +397,21 @@
 
     kk = project(pl.ds(1536, 256))
     vv = project(pl.ds(1792, 256))
-    kv[pl.ds(blk, 1), :, pl.ds(0, 128)] = turned(kk[:, :128])[None]
-    kv[pl.ds(blk, 1), :, pl.ds(128, 128)] = turned(kk[:, 128:])[None]
-    kv[pl.ds(blk, 1), :, pl.ds(256, 256)] = vv.astype(BF)[None]
-    kvs = [send(kv.at[blk], blk_dev((blk + k) % 8)) for k in range(1, 8)]
+    near[4, :, 0:128] = turned(kk[:, :128])
+    near[4, :, 128:256] = turned(kk[:, 128:])
+    near[4, :, 256:512] = vv.astype(BF)
+    base = net.take(16)
+    close_kv, far_kv = {}, {}
+    for k in range(1, 8):
+        to = blk_dev((blk + k) % 8)
+        far_kv[k] = net.make(near.at[4], kv.at[blk], to, base + k)
+        if k < 5:
+            close_kv[k] = net.make(near.at[4], near.at[4 - k], to, base + 8 + k)
+
+            @pl.when(blk + k < 8)
+            def _(k=k):
+                close_kv[k].start()
+
 
     def query(n, carry):
         p = project(pl.ds(pl.multiple_of(n * 256, 256), 256))
@@ -333,16 +420,23 @@
         return carry
 
     lax.fori_loop(0, 6, query, 0)
+    for cp in i1:
+        cp.wait_recv()
+    i3 = {k: [send(w.at[:, y, 1 - xl, c], net.dev(y=k)) for w in (wi, wo)] for k in (1, 3)}
+    p5 += [send(w.at[:, y, 1 - xl, c], net.dev(c=1)) for w in (wi, wo)]
     up, down = net.dev(y=1), net.dev(y=3)
     lo, hi = (y + 3) % 4, (y + 1) % 4
-    for cp in kvs:
-        cp.wait_recv()
-    pages[...] = kv[table[0, 0]]
+    for k in range(1, 5):
+
+        @pl.when(blk >= k)
+        def _(k=k):
+            close_kv[k].wait_recv()
+
 
     def attend(h, carry):
         g = h // 6
-        k = kv[pl.ds(low, 5), :, pl.ds(pl.multiple_of(g * 128, 128), 128)].reshape(640, 128)
-        v = kv[pl.ds(low, 5), :, pl.ds(pl.multiple_of(256 + g * 128, 128), 128)].reshape(640, 128)
+        k = near[:, :, pl.ds(pl.multiple_of(g * 128, 128), 128)].reshape(640, 128)
+        v = near[:, :, pl.ds(pl.multiple_of(256 + g * 128, 128), 128)].reshape(640, 128)
         s = lax.dot_general(qh[h], k, (((1,), (1,)), ((), ())), preferred_element_type=F32)
         s = jnp.where(msk[...] > 0, s * (1.0 / math.sqrt(HD)), -1e30)
         w = jnp.exp(s - jnp.max(s, axis=-1, keepdims=True))
@@ -352,45 +446,41 @@
         return carry
 
     lax.fori_loop(0, 12, attend, 0)
-    for n, k in enumerate(xs):
-        m4[n].wait_recv()
-        zf = (z + 4 - k) % 4
-        col = pl.ds(pl.multiple_of(zf * 384, 128), 384)
-        m5.append(send(wm.at[:, :, c, :, :, col], net.dev(c=1)))
-    for k in (1, 3):
-        i2[k].wait_recv()
-    for k in (1, 3):
-        i3[k].wait_recv()
-    r4 = [send(wi.at[:, lo, 0, c], up), send(wi.at[:, hi, 1, c], down)]
-    p6 = [send(wi.at[:, lo, :, c], net.dev(c=1)), send(wi.at[:, hi, :, c], net.dev(c=1))]
-    for cp in m5:
-        cp.wait_recv()
+    for n in range(3):
+        for m in mc:
+            m.land(n)
+    for m in mc:
+        m.close()
 
     def mix(n, carry):
         col = pl.ds(pl.multiple_of(n * 256, 256), 256)
         w = wm[:, :, :, :, :, col].reshape(D, 256)
-        hid[:, col] = tokens[:, col].astype(F32) + jnp.dot(
+        hid[:, col] = tk[:, col].astype(F32) + jnp.dot(
             at[...], w, preferred_element_type=F32
         )
         return carry
 
     lax.fori_loop(0, 6, mix, 0)
-    rows[pl.ds(blk, 1)] = scaled(hid[...], gain_m[...])[None]
+    rows[pl.ds(blk, 1)] = scaled(hid[...], gain_m[...].reshape(1, D))[None]
     across = net.dev(x=2)
     t1 = {k: send(rows.at[blk], net.dev(z=k)) for k in xs}
     tx = send(rows.at[blk], across)
 
-    for k in xs:
-        u1[k].wait_recv()
-        yf = (y + 4 - k) % 4
-        u2.append(send(wo.at[:, yf, xl, c], net.xflip()))
-        p6.append(send(wo.at[:, yf, xl, c], net.dev(c=1)))
-    for n, k in enumerate((0,) + xs):
-        u2[n].wait_recv()
-        p6.append(send(wo.at[:, (y + 4 - k) % 4, 1 - xl, c], net.dev(c=1)))
-    for cp in r4:
-        cp.wait_recv()
-    p6.append(send(wi.at[:, (y + 2) % 4, :, c], net.dev(c=1)))
+    for k in range(1, 8):
+        if k > 4:
+            far_kv[k].start()
+            continue
+
+        @pl.when(blk + k >= 8)
+        def _(k=k):
+            far_kv[k].start()
+
+    for k in (1, 3):
+        for cp in i2[k] + i3[k]:
+            cp.wait_recv()
+    r4 = [send(w.at[:, lo, 0, c], up) for w in (wi, wo)]
+    r4 += [send(w.at[:, hi, 1, c], down) for w in (wi, wo)]
+    p6 = [send(w.at[:, v, :, c], net.dev(c=1)) for w in (wi, wo) for v in (lo, hi)]
     tx.wait_recv()
     blk_x = z * 2 + 1 - xh
     t2 = {k: send(rows.at[blk_x], net.dev(z=k)) for k in (1, 3)}
@@ -399,6 +489,9 @@
     t3 = send(rows.at[blk_o], across)
     for k in (1, 3):
         t1[k].wait_recv()
+    for cp in r4:
+        cp.wait_recv()
+    p6 += [send(w.at[:, (y + 2) % 4, :, c], net.dev(c=1)) for w in (wi, wo)]
     for cp in p5 + p6:
         cp.wait_recv()
 
@@ -479,6 +572,33 @@
         cp.wait_recv()
     pb[0] = (pb[0].astype(F32) + rb[0].astype(F32) + rb[1].astype(F32)).astype(BF)
     s5 = send(pb.at[0], across, rx.at[1])
+    kv[pl.ds(blk, 1)] = near[4][None]
+    for k in range(1, 8):
+        if k > 4:
+            far_kv[k].wait_recv()
+            far_kv[k].wait_send()
+            continue
+
+        @pl.when(blk < k)
+        def _(k=k):
+            far_kv[k].wait_recv()
+
+        @pl.when(blk >= k)
+        def _(k=k):
+            kv[pl.ds(blk - k, 1)] = near[4 - k][None]
+
+        @pl.when(blk + k < 8)
+        def _(k=k):
+            close_kv[k].wait_send()
+
+        @pl.when(blk + k >= 8)
+        def _(k=k):
+            far_kv[k].wait_send()
+
+    logical = jnp.int32(0)
+    for i in range(8):
+        logical = jnp.where(table[0, i] == blk, i, logical)
+    pages[...] = kv[logical]
     s4.wait_recv()
     s5.wait_recv()
     mixed[...] = (hid[...] + rz[...].astype(F32) + rx[1].astype(F32)).astype(BF)
@@ -504,21 +624,31 @@
             jax.ShapeDtypeStruct((128, D), BF),
             jax.ShapeDtypeStruct((128, 512), BF),
         ),
-        in_specs=[vm] * 8 + [sm] * 2,
+        in_specs=[pl.BlockSpec(memory_space=pl.ANY)] * 5 + [vm] * 3 + [sm] * 2,
         out_specs=(vm,) * 2,
         scratch_shapes=[
             pltpu.VMEM((4, 2, 2, 2, 48, 2048), BF),
             pltpu.VMEM((4, 2, 2, 2, 48, D), BF),
             pltpu.VMEM((2, 4, 2, 2, 96, D), BF),
             pltpu.VMEM((2, 4, 2, 2, 48, D), BF),
+            pltpu.VMEM((12, 2048), F32),
+            pltpu.VMEM((12, D), F32),
+            pltpu.VMEM((12, 16, D), F32),
+            pltpu.VMEM((6, 16, D), F32),
+            pltpu.VMEM((128, D), BF),
             pltpu.VMEM((4, 12, 512), BF),
             pltpu.VMEM((4, 12, 384), BF),
-            pltpu.VMEM((8, 2, 12, D), BF),
-            pltpu.VMEM((8, 2, 6, D), BF),
+            pltpu.VMEM((8, 24, D), BF),
+            pltpu.VMEM((8, 24, FF), BF),
+            pltpu.VMEM((4, 12, 512), BF),
+            pltpu.VMEM((4, 12, 384), BF),
+            pltpu.VMEM((8, 24, D), BF),
+            pltpu.VMEM((8, 24, FF), BF),
             pltpu.VMEM((8, 2, 128), F32),
             pltpu.VMEM((128, D), BF),
             pltpu.VMEM((12, 128, 128), BF),
             pltpu.VMEM((8, 128, 512), BF),
+            pltpu.VMEM((5, 128, 512), BF),
             pltpu.VMEM((128, D), BF),
             pltpu.VMEM((128, D), F32),
             pltpu.VMEM((8, 128, D), BF),
@@ -534,8 +664,9 @@
             pltpu.VMEM((2, 128, D), BF),
             pltpu.VMEM((2, 128, D), BF),
             pltpu.VMEM((128, D), BF),
-            pltpu.SemaphoreType.DMA((160,)),
-            pltpu.SemaphoreType.DMA((160,)),
+            pltpu.SemaphoreType.DMA((5,)),
+            pltpu.SemaphoreType.DMA((200,)),
+            pltpu.SemaphoreType.DMA((200,)),
         ],
         compiler_params=pltpu.CompilerParams(
             collective_id=0, has_side_effects=True, vmem_limit_bytes=64 << 20
@@ -556,9 +687,6 @@
     routes,
     gates,
 ):
-    place = lax.axis_index("blk")
-    qs = attn_in.astype(BF).reshape(12, 2, 4, 256).transpose(2, 0, 1, 3).reshape(4, 12, 512)
-    ms = attn_out.astype(BF).reshape(12, 4, 384).transpose(1, 0, 2)
     ids = jnp.arange(E, dtype=jnp.int32)
     weight = jnp.sum(
         jnp.where(
@@ -566,19 +694,17 @@
         ),
         axis=1,
     ).reshape(8, 2, 128)
-    page_ids = jnp.arange(8, dtype=jnp.int32)
-    logical = jnp.sum(jnp.where(page_table == place, page_ids[None, :], 0), axis=1, keepdims=True)
     mixed, pages = layer_call(
-        qs,
-        ms,
-        expert_in.astype(BF),
-        expert_out.astype(BF),
+        attn_in,
+        attn_out,
+        expert_in.transpose(1, 0, 2),
+        expert_out.transpose(1, 0, 2),
+        tokens,
         weight,
-        tokens,
-        attn_gain[None],
-        moe_gain[None],
+        attn_gain,
+        moe_gain,
         lengths,
-        logical,
+        page_table,
     )
     return mixed, pages[None]
 

time: 193 us -> 178 us (0.922); the launches traced: 193 us -> 176 us
  Pallas kernels: 182 us -> 170 us
  local copies, waits for them, and re-layouts: 8.11 us -> 3.33 us
    pallas_call x1, Pallas kernels: 182 us -> 170 us  [layer_call(): pl.pallas_call(layer_kernel, out_shape=(jax.ShapeDtypeStruct((128, D), BF...]
    convert_element_type x2 -> x0, local copies, waits for them, and re-layouts: 2.14 us -> none  [the longest x1 1.23 us: body(): expert_in.astype(BF)]
where the time goes in v3:
time: 178 us; the launch traced here: 176 us
  Pallas kernels  170 us (96%)
  local copies, waits for them, and re-layouts  3.33 us (2%)
  other arithmetic  1.97 us (1%)
    pallas_call x1, Pallas kernels, layer_call(): pl.pallas_call(layer_kernel, out_shape=(jax.ShapeDtypeStruct((128, D), BF...  170 us

profile of v3, /device:TPU:96, one launch (start us, length us, event | category | flops | bytes accessed | tf_op | source)
XLA Modules:
  0.0 176.2 jit_solution(2336473333093281212)
XLA Ops:
  0.6 0.7 convert_bitcast_fusion
  1.3 1.3 select_reduce_fusion
  2.6 170.2 %shard_map.122 = (bf16[128,1536]{1,0:T(8,128)(2,1)}, bf16[128,512]{1,0:T(8,128)(2,1)}) custom-call(f32[12,2048]{1,0:T(8,128)} %xq.1, f32[12,1536]{1,0:T(8,128)} %xm.1, f32[12,16,1536]{2,1,0:T(8,128)} %bitcast.7, f32[6,16,1536]{2,1,0:T(8,128)} %bitcast.8, bf16[128,1536]{1,0:T(8,128)(2,1)} %tokens.1, f32[8,2,128]{2,1,0:T(2,128)} %bitcast.10, f32[1536]{0:T(1024)} %gain_a.1, ...), custom_call_target="tpu_custom_call" | custom-call | tf_op jit(solution)/shard_map/pallas_call | solution.py:621
  172.8 1.8 %copy.15 = bf16[128,1536]{1,0:T(8,128)(2,1)} copy(bf16[128,1536]{1,0:T(8,128)(2,1)} %get-tuple-element.8) | data formatting | bytes 786432
  174.6 1.6 copy.16

commit v4 on v3

--- a/solution.py
+++ b/solution.py
@@ -286,7 +286,7 @@
             for cp in self.chip:
                 cp.wait_recv()
 
-    qc = [Color(wq, 512, 256, "xzy"), Color(wq, 0, 128, "xyz"), Color(wq, 1536, 128, "yzx")]
+    qc = [Color(wq, 512, 256, "xyz"), Color(wq, 0, 128, "xzy"), Color(wq, 1536, 128, "yzx")]
     mc = [Color(wm, 512, 256, "yzx"), Color(wm, 0, 128, "xyz")]
     wait_first(qs, q1, 0)
     block = stack([q1[j] for j in range(4)])

time: 178 us -> 176 us (0.989)
  no operation moved by 1% of the time
where the time goes in v4:
time: 176 us; the launch traced here: 175 us
  Pallas kernels  169 us (96%)
  local copies, waits for them, and re-layouts  3.33 us (2%)
  other arithmetic  1.97 us (1%)
    pallas_call x1, Pallas kernels, layer_call(): pl.pallas_call(layer_kernel, out_shape=(jax.ShapeDtypeStruct((128, D), BF...  169 us

profile of v4, /device:TPU:96, one launch (start us, length us, event | category | flops | bytes accessed | tf_op | source)
XLA Modules:
  0.0 174.5 jit_solution(11785890185885414064)
XLA Ops:
  0.6 0.7 convert_bitcast_fusion
  1.3 1.3 select_reduce_fusion
  2.6 168.6 %shard_map.122 = (bf16[128,1536]{1,0:T(8,128)(2,1)}, bf16[128,512]{1,0:T(8,128)(2,1)}) custom-call(f32[12,2048]{1,0:T(8,128)} %xq.1, f32[12,1536]{1,0:T(8,128)} %xm.1, f32[12,16,1536]{2,1,0:T(8,128)} %bitcast.7, f32[6,16,1536]{2,1,0:T(8,128)} %bitcast.8, bf16[128,1536]{1,0:T(8,128)(2,1)} %tokens.1, f32[8,2,128]{2,1,0:T(2,128)} %bitcast.10, f32[1536]{0:T(1024)} %gain_a.1, ...), custom_call_target="tpu_custom_call" | custom-call | tf_op jit(solution)/shard_map/pallas_call | solution.py:621
  171.2 1.8 %copy.15 = bf16[128,1536]{1,0:T(8,128)(2,1)} copy(bf16[128,1536]{1,0:T(8,128)(2,1)} %get-tuple-element.8) | data formatting | bytes 786432
  173.0 1.6 copy.16

commit v5 on v4

--- a/solution.py
+++ b/solution.py
@@ -433,6 +433,15 @@
             close_kv[k].wait_recv()
 
 
+    for k in range(1, 8):
+        if k > 4:
+            far_kv[k].start()
+            continue
+
+        @pl.when(blk + k >= 8)
+        def _(k=k):
+            far_kv[k].start()
+
     def attend(h, carry):
         g = h // 6
         k = near[:, :, pl.ds(pl.multiple_of(g * 128, 128), 128)].reshape(640, 128)
@@ -465,15 +474,6 @@
     across = net.dev(x=2)
     t1 = {k: send(rows.at[blk], net.dev(z=k)) for k in xs}
     tx = send(rows.at[blk], across)
-
-    for k in range(1, 8):
-        if k > 4:
-            far_kv[k].start()
-            continue
-
-        @pl.when(blk + k >= 8)
-        def _(k=k):
-            far_kv[k].start()
 
     for k in (1, 3):
         for cp in i2[k] + i3[k]:

time: 176 us -> 174 us (0.989)
  the two profiles are of different devices: /device:TPU:96 before, /device:TPU:24 now
where the time goes in v5:
time: 174 us; the launch traced here: 173 us
  Pallas kernels  167 us (96%)
  local copies, waits for them, and re-layouts  3.33 us (2%)
  other arithmetic  1.97 us (1%)
    pallas_call x1, Pallas kernels, layer_call(): pl.pallas_call(layer_kernel, out_shape=(jax.ShapeDtypeStruct((128, D), BF...  167 us

profile of v5, /device:TPU:24, one launch (start us, length us, event | category | flops | bytes accessed | tf_op | source)
XLA Modules:
  0.0 173.2 jit_solution(4953950727944491706)
XLA Ops:
  0.6 0.7 convert_bitcast_fusion
  1.3 1.3 select_reduce_fusion
  2.6 167.3 %shard_map.122 = (bf16[128,1536]{1,0:T(8,128)(2,1)}, bf16[128,512]{1,0:T(8,128)(2,1)}) custom-call(f32[12,2048]{1,0:T(8,128)} %xq.1, f32[12,1536]{1,0:T(8,128)} %xm.1, f32[12,16,1536]{2,1,0:T(8,128)} %bitcast.7, f32[6,16,1536]{2,1,0:T(8,128)} %bitcast.8, bf16[128,1536]{1,0:T(8,128)(2,1)} %tokens.1, f32[8,2,128]{2,1,0:T(2,128)} %bitcast.10, f32[1536]{0:T(1024)} %gain_a.1, ...), custom_call_target="tpu_custom_call" | custom-call | tf_op jit(solution)/shard_map/pallas_call | solution.py:621
  169.9 1.8 %copy.15 = bf16[128,1536]{1,0:T(8,128)(2,1)} copy(bf16[128,1536]{1,0:T(8,128)(2,1)} %get-tuple-element.8) | data formatting | bytes 786432
  171.7 1.6 copy.16
